TPU v7x, 32 devices: a whole 2x2x4 slice. The times are simulated.
32 devices in a mesh: depth: 2 (over y), lat: 8 (over z, x), freq: 2 (over core).
Axes of the slice: x: 2, y: 2, z: 4, core: 2. Of those that a mesh axis runs over, the one named last changes fastest.
Arguments:
- surface: bfloat16 [6, 2, 128, 8192], P('freq', None, None, 'lat'), may hold values from -6 to 6
- refl: float32 [2, 8192], P('depth', 'lat'), may hold values from -0.5 to 0.5
- pool: bfloat16 [2, 6, 8, 128, 256], P('depth', 'freq'), may hold values from -0.375 to 0.375
- tile_ids: int32 [2, 64, 10], P('depth', 'lat'), may hold values from 0 to 63, as said below
- block_ids: int32 [2, 64, 10], P('depth', 'lat'), may hold values from 0 to 7
- counts: int32 [2, 64], P('depth', 'lat'), may hold values from 1 to 10, as said below
Outputs:
- image: float32 [2, 8192], P('depth', 'lat')
Inputs may be any that keep to these rules, and one draw needn't show every extreme that they name: tile_ids[l, j, k] = (j + o) mod 64 for an offset o with -8 <= o <= 8; slot 0 names the row's own tile; in every level some row has all 10 slots live with offsets 8 at slot 1 and -8 at slot 2. Slots k >= counts[l, j] of row j are padding; in every level some row has all 10 slots live.
All inputs are finite; a program needn't handle non-finite values.
Results may differ from a plain program's by a relative error of at most 0.00055.
Values may be sent and summed in bfloat16 or wider, within the bound.
No kernel may reach another device: no remote copies, remote signals or barrier semaphores. Data moves between devices by JAX's collectives and lax.ppermute only.
A program may use at most 128 MiB of HBM per device.

v0:
```python
import functools

import jax
import jax.numpy as jnp
from jax import lax
from jax.experimental import pallas as pl
from jax.experimental.pallas import tpu as pltpu
from jax.sharding import PartitionSpec as P


TILE = 128
TILE_DEV = 8


def extended_2(block, sides, width):
    for axis, dim in sides:
        count = lax.axis_size(axis)
        forward = [(i, i + 1) for i in range(count - 1)]
        forward.append((count - 1, 0))
        backward = [(target, source) for source, target in forward]
        low = lax.ppermute(
            lax.slice_in_dim(block, block.shape[dim] - width, None, axis=dim), axis, forward
        )
        high = lax.ppermute(lax.slice_in_dim(block, 0, width, axis=dim), axis, backward)
        block = jnp.concatenate([low, block, high], axis=dim)
    return block


def aperture_rim(wave_field):
    return extended_2(wave_field, (("lat", 3),), TILE_DEV * TILE)


def extrapolate(extended, pool_level, local_ids, block_level, count_level, refl_level):
    freqs_here = extended.shape[0]
    shot_rows = extended.shape[2]
    tile_rows = local_ids.shape[0]
    slot_total = local_ids.shape[1]
    tile_grid = extended.reshape(freqs_here, 2, shot_rows, -1, TILE)
    slot_live = (jnp.arange(slot_total)[None, :] < count_level[:, None]).astype(jnp.bfloat16)
    picked = jnp.take(tile_grid, local_ids, axis=3) * slot_live[None, None, None, :, :, None]
    chosen = jnp.take(pool_level, block_level, axis=1)
    product = jnp.einsum("fsarkt,frktc->rfsac", picked, chosen, preferred_element_type=jnp.float32)
    real_part = product[:, :, 0, :, :TILE] - product[:, :, 1, :, TILE:]
    imag_part = product[:, :, 0, :, TILE:] + product[:, :, 1, :, :TILE]
    row_scale = 1.0 / jnp.sqrt(count_level.astype(jnp.float32))
    rows_out = jnp.stack([real_part, imag_part], 2) * row_scale[:, None, None, None, None]
    wave_out = jnp.transpose(rows_out, (1, 2, 3, 0, 4)).reshape(
        freqs_here, 2, shot_rows, tile_rows * TILE
    )
    wave_out = wave_out * (1.0 - refl_level)
    return (wave_out.astype(jnp.bfloat16), jnp.sum(wave_out * wave_out, axis=(0, 1, 2)))


def per_device(surface, refl, pool, tile_ids, block_ids, counts):
    depth_index = lax.axis_index("depth")
    lat_index = lax.axis_index("lat")
    tile_count = TILE_DEV * lax.axis_size("lat")
    first_tile = lat_index * TILE_DEV - TILE_DEV
    freqs_here = surface.shape[0]
    shot_total = surface.shape[2]
    lateral_width = surface.shape[3]
    shot_rows = shot_total // lax.axis_size("depth")
    own_shots = lax.dynamic_slice_in_dim(surface, depth_index * shot_rows, shot_rows, 2)
    pool_all = lax.all_gather(pool, "depth", axis=0, tiled=True)
    ids_all, blocks_all, counts_all = (
        lax.all_gather(tile_ids, "depth", axis=0, tiled=True),
        lax.all_gather(block_ids, "depth", axis=0, tiled=True),
        lax.all_gather(counts, "depth", axis=0, tiled=True),
    )
    refl_all = lax.all_gather(refl, "depth", axis=0, tiled=True)
    level_total = pool_all.shape[0]

    def level_step(level_index, loop_state):
        wave_field, images = loop_state
        ids_here = lax.dynamic_index_in_dim(ids_all, level_index, 0, keepdims=False)
        local_level = jnp.mod(ids_here - first_tile, tile_count)
        pool_here = lax.dynamic_index_in_dim(pool_all, level_index, 0, keepdims=False)
        blocks_here = lax.dynamic_index_in_dim(blocks_all, level_index, 0, keepdims=False)
        counts_here = lax.dynamic_index_in_dim(counts_all, level_index, 0, keepdims=False)
        refl_here = lax.dynamic_index_in_dim(refl_all, level_index, 0, keepdims=False)
        handed, partial_value = extrapolate(
            aperture_rim(wave_field), pool_here, local_level, blocks_here, counts_here, refl_here
        )
        images = lax.dynamic_update_index_in_dim(images, partial_value, level_index, 0)
        return (handed, images)

    start_images = jnp.zeros((level_total, lateral_width), jnp.float32)
    loop_state = lax.fori_loop(0, level_total, level_step, (own_shots, start_images))
    image_local = lax.psum_scatter(loop_state[1], "depth", scatter_dimension=0, tiled=True)[0]
    summed = lax.psum(image_local, "freq")
    divisor = freqs_here * lax.axis_size("freq") * shot_total
    return (summed / divisor)[None, :]


ROWS_STEP = 4
LANES = 128
SUBLANES = 8
HALF = LANES // 2
PACKED = 16
VMEM_SPACE = pl.BlockSpec(memory_space=pltpu.VMEM)
SMEM_SPACE = pl.BlockSpec(memory_space=pltpu.SMEM)
ANY_SPACE = pl.BlockSpec(memory_space=pl.ANY)


def table_kernel(
    depth_ref, pool_ref, refl_ref, tiles_ref, blocks_ref, counts_ref, out_ref, own_ref, half_ref, sems
):
    copies = [
        pltpu.make_async_copy(pool_ref.at[0, 2 * (1 - depth_ref[0])], own_ref, sems.at[0]),
        pltpu.make_async_copy(pool_ref.at[0, 1], half_ref, sems.at[1]),
    ]
    for copy in copies:
        copy.start()
    rows = tiles_ref.shape[1]
    slots = tiles_ref.shape[2]
    for row in range(rows):
        out_ref[row:row + 1, :] = refl_ref[:, row * LANES:(row + 1) * LANES]
    out_ref[rows:, :] = jnp.zeros((rows, LANES), jnp.float32)
    out_ref[rows:, :slots] = blocks_ref[0].astype(jnp.float32)
    out_ref[rows:, slots:2 * slots] = tiles_ref[0].astype(jnp.float32)
    spread = jnp.broadcast_to(counts_ref[...].astype(jnp.float32), (rows, rows))
    across = lax.broadcasted_iota(jnp.int32, (rows, rows), 1)
    down = lax.broadcasted_iota(jnp.int32, (rows, rows), 0)
    column = jnp.sum(jnp.where(across == down, spread, 0.0), axis=1, keepdims=True)
    out_ref[rows:, 2 * slots:2 * slots + 1] = column
    for copy in copies:
        copy.wait()


def front_kernel(lat_size, depth_ref, lat_ref, surface_ref, mine_ref, other_ref, *refs):
    outs, sems = refs[:-1], refs[-1]
    depth_index = depth_ref[0]
    groups = surface_ref.shape[2] // lat_size
    height = surface_ref.shape[3]
    rows = height // SUBLANES
    copies = []
    for turn, out in enumerate(outs, 1):
        target = lax.rem(lat_ref[0] + turn, lat_size)
        sources = [
            surface_ref.at[2 * depth_index, part, groups * target + group]
            for part in range(2)
            for group in range(groups)
        ] + [surface_ref.at[1, part, depth_index * lat_size + target] for part in range(2)]
        copies += [
            pltpu.make_async_copy(
                source, out.at[pl.ds(place * height, height), :], sems.at[turn - 1, place]
            )
            for place, source in enumerate(sources)
        ]
    for copy in copies:
        copy.start()
    first = jnp.where(depth_index == 0, mine_ref[...], other_ref[...])
    second = jnp.where(depth_index == 0, other_ref[rows:, :], mine_ref[rows:, :])
    refl = first[:rows]
    high = refl.astype(jnp.bfloat16)
    low = (refl - high.astype(jnp.float32)).astype(jnp.bfloat16)
    lists = first[rows:] + pltpu.roll(second, HALF, 1)
    pair = jnp.concatenate([high.astype(jnp.float32), low.astype(jnp.float32)], axis=0)
    for out in outs:
        start = out.shape[0] - 3 * rows
        out[start:start + 2 * rows, :] = pair.astype(jnp.bfloat16)
        out[start + 2 * rows:, :] = lists.astype(jnp.bfloat16)
    for copy in copies:
        copy.wait()


def level_kernel(lat_size, freq_size, slots, levels, depth_ref, lat_ref, *refs):
    wave_refs = refs[:lat_size]
    (local_ref, remote_own_ref, remote_half_ref, image_ref, table, own_buf, half_buf, squares_buf,
     lists_buf, factor_buf, index_buf, index_ref, sem) = refs[lat_size:]
    blocks = remote_own_ref.shape[0]
    entries = factor_buf.shape[1]
    rows = entries // lat_size
    own = own_buf.shape[0] // entries
    half = own // 2
    unit = 2 * (own + half)
    depth_index = depth_ref[0]
    for turn, wave in enumerate(wave_refs):
        source = lax.rem(lat_ref[0] + lat_size - turn, lat_size)
        top = wave.shape[0] - 3 * rows
        pair = wave[top:top + 2 * rows, :].astype(jnp.float32)
        high, low = pair[:rows], pair[rows:]
        lists = wave[top + 2 * rows:, :].astype(jnp.float32)
        start = pl.multiple_of(source * rows, rows)
        factor_buf[0, pl.ds(start, rows), :] = 1.0 - (high + low)
        lists_buf[pl.ds(start, rows), :] = lists
    lane = lax.broadcasted_iota(jnp.int32, (entries, LANES), 1).astype(jnp.float32)
    for level in range(levels):
        listed = lists_buf[...]
        if level:
            listed = pltpu.roll(listed, LANES - HALF, 1)
        count = jnp.broadcast_to(listed[:, 2 * slots:2 * slots + 1], (entries, LANES))
        tile = pltpu.roll(listed, LANES - slots, 1)
        place = jnp.where(lane < count, listed * entries + tile, float(blocks * entries))
        index_buf[level] = (place * unit).astype(jnp.int32)
        scale = 1.0 / jnp.sqrt(count)
        factor_buf[level] = scale if level == levels - 1 else scale * factor_buf[level]
    index_copy = pltpu.make_async_copy(index_buf, index_ref, sem)
    index_copy.start()
    table[blocks * entries * unit:, :] = jnp.zeros((unit, LANES), jnp.float32)

    for turn, wave in enumerate(wave_refs):
        source = lax.rem(lat_ref[0] + lat_size - turn, lat_size)

        height = rows * SUBLANES
        for part in range(2):
            lanes = slice(part * LANES, (part + 1) * LANES)
            for group in range(2):
                start = pl.multiple_of((source * 2 + group) * height, height)
                place = (part * 2 + group) * height
                own_buf[pl.ds(start, height), lanes] = wave[place:place + height, :]
            start = pl.multiple_of(source * height, height)
            place = (4 + part) * height
            half_buf[pl.ds(start, height), lanes] = wave[place:place + height, :]

    def weights_of(level, local, remote):
        upper = jnp.where(depth_index == level, local, remote)
        lower = jnp.concatenate([-upper[:, TILE:], upper[:, :TILE]], axis=1)
        return jnp.concatenate([upper, lower], axis=0)

    def units(product, groups):
        sources = lat_size if groups else 1
        product = product.reshape(sources, max(groups, 1), entries // sources, -1, 2 * TILE)
        return [
            product[:, group, :, :, part * TILE:(part + 1) * TILE].reshape(entries, -1, TILE)
            for part in range(2)
            for group in range(max(groups, 1))
        ]

    for level in range(levels):
        last = level == levels - 1

        def block_step(block, carry):
            weights_own = weights_of(
                level, local_ref[0, 2 * depth_index, block], remote_own_ref[block]
            )
            weights_half = weights_of(level, local_ref[0, 1, block], remote_half_ref[block])
            product_own = jnp.dot(own_buf[...], weights_own, preferred_element_type=jnp.float32)
            product_half = jnp.dot(half_buf[...], weights_half, preferred_element_type=jnp.float32)
            joined = units(product_own, 0 if level else own // SUBLANES) + units(product_half, 0)
            start = pl.multiple_of(block * entries * unit, entries * unit)
            table[pl.ds(start, entries * unit), :] = jnp.concatenate(joined, axis=1).reshape(
                entries * unit, LANES
            )
            return carry

        lax.fori_loop(0, blocks, block_step, 0, unroll=4)
        if level == 0:
            index_copy.wait()

        def row_step(step, carry):
            outs = []
            for inner in range(ROWS_STEP):
                row = step * ROWS_STEP + inner
                total = None
                for slot in range(slots):
                    start = pl.multiple_of(index_ref[level, row, slot], SUBLANES)
                    term = table[pl.ds(start, unit), :]
                    total = term if total is None else total + term
                total = total * factor_buf[level, pl.ds(row, 1), :]
                outs.append(total)
                squares = total * total
                squares_buf[level * entries + row] = jnp.sum(
                    squares.reshape(unit // SUBLANES, SUBLANES, LANES), axis=0
                )
            if not last:
                for k, out in enumerate(outs):
                    start = pl.multiple_of((step * ROWS_STEP + k) * own, own)
                    own_buf[pl.ds(start, own), :] = jnp.concatenate(
                        [out[:own], out[own:2 * own]], axis=1
                    ).astype(jnp.bfloat16)
                for k in range(0, ROWS_STEP, 2):
                    pair = outs[k:k + 2]
                    real = jnp.concatenate([out[2 * own:2 * own + half] for out in pair], axis=0)
                    imag = jnp.concatenate([out[2 * own + half:] for out in pair], axis=0)
                    start = pl.multiple_of((step * ROWS_STEP + k) * half, 2 * half)
                    half_buf[pl.ds(start, 2 * half), :] = jnp.concatenate(
                        [real, imag], axis=1
                    ).astype(jnp.bfloat16)
            return carry

        lax.fori_loop(0, entries // ROWS_STEP, row_step, 0)

    summed = jnp.sum(squares_buf[...], axis=1)
    for level in range(levels):
        for target in range(lat_size):
            start = level * entries + target * rows
            for copy in range(freq_size):
                image_ref[level, target, copy] = summed[start:start + rows]


def per_device_fast(surface, refl, pool, tile_ids, block_ids, counts):
    depth_index = lax.axis_index("depth")
    lat_index = lax.axis_index("lat")
    levels = lax.axis_size("depth")
    lat_size = lax.axis_size("lat")
    freq_size = lax.axis_size("freq")
    freqs_here, _, shot_total, lateral_width = surface.shape
    rows, slots = tile_ids.shape[1:]
    blocks = pool.shape[2]
    entries = rows * lat_size
    own = shot_total // lat_size
    half = own // 2
    swap = [(0, 1), (1, 0)]
    depth_id = depth_index.astype(jnp.int32).reshape(1)
    lat_id = lat_index.astype(jnp.int32).reshape(1)

    sent = jax.ShapeDtypeStruct(pool.shape[2:], pool.dtype)
    mine, send_own, send_half = pl.pallas_call(
        table_kernel,
        out_shape=[jax.ShapeDtypeStruct((2 * rows, LANES), jnp.float32), sent, sent],
        in_specs=[SMEM_SPACE, ANY_SPACE] + [VMEM_SPACE] * 4,
        out_specs=[VMEM_SPACE] * 3,
        scratch_shapes=[pltpu.SemaphoreType.DMA((2,))],
        name="tables",
    )(depth_id, pool, refl, tile_ids, block_ids, counts)
    other = lax.ppermute(mine, "depth", swap)
    remote_own = lax.ppermute(send_own, "depth", swap)
    remote_half = lax.ppermute(send_half, "depth", swap)

    pieces = surface.reshape(
        freqs_here, 2, shot_total // SUBLANES, SUBLANES, rows, LANES
    ).transpose(0, 1, 2, 4, 3, 5).reshape(
        freqs_here, 2, shot_total // SUBLANES, rows * SUBLANES, LANES
    )
    height = (2 * (own + half) + 3) * rows
    chunks = pl.pallas_call(
        functools.partial(front_kernel, lat_size),
        out_shape=[jax.ShapeDtypeStruct((height, LANES), jnp.bfloat16)] * (lat_size - 1),
        in_specs=[SMEM_SPACE] * 2 + [ANY_SPACE] + [VMEM_SPACE] * 2,
        out_specs=[VMEM_SPACE] * (lat_size - 1),
        scratch_shapes=[pltpu.SemaphoreType.DMA((lat_size - 1, 2 * (own + half) // SUBLANES))],
        name="front",
    )(depth_id, lat_id, pieces, mine, other)
    own_pieces = lax.dynamic_slice(
        pieces, (2 * depth_index, 0, lat_index * (own // SUBLANES), 0, 0),
        (1, 2, own // SUBLANES, rows * SUBLANES, LANES),
    )
    half_pieces = lax.dynamic_slice(
        pieces, (1, 0, depth_index * lat_size + lat_index, 0, 0), (1, 2, 1, rows * SUBLANES, LANES)
    )
    stay = jnp.concatenate(
        [part.reshape(-1, LANES) for part in (own_pieces, half_pieces)]
        + [chunks[0][height - 3 * rows:]], axis=0,
    )
    middle = lat_size // 2
    order = sorted(range(1, lat_size), key=lambda turn: abs(turn - middle))
    waves = [stay] + [None] * (lat_size - 1)
    for turn in order:
        around = [(source, (source + turn) % lat_size) for source in range(lat_size)]
        waves[turn] = lax.ppermute(chunks[turn - 1], "lat", around)

    spread = pl.pallas_call(
        functools.partial(level_kernel, lat_size, freq_size, slots, levels),
        out_shape=jax.ShapeDtypeStruct((levels, lat_size, freq_size, rows, LANES), jnp.float32),
        in_specs=[SMEM_SPACE] * 2 + [VMEM_SPACE] * (lat_size + 3),
        out_specs=VMEM_SPACE,
        scratch_shapes=[
            pltpu.VMEM(((blocks * entries + 1) * 2 * (own + half), LANES), jnp.float32),
            pltpu.VMEM((entries * own, 2 * TILE), jnp.bfloat16),
            pltpu.VMEM((entries * half, 2 * TILE), jnp.bfloat16),
            pltpu.VMEM((levels * entries, SUBLANES, LANES), jnp.float32),
            pltpu.VMEM((entries, LANES), jnp.float32),
            pltpu.VMEM((levels, entries, LANES), jnp.float32),
            pltpu.VMEM((levels, entries, LANES), jnp.int32),
            pltpu.SMEM((levels, entries, LANES), jnp.int32),
            pltpu.SemaphoreType.DMA,
        ],
        cost_estimate=pl.CostEstimate(
            flops=8 * levels * blocks * entries * (own + half) * TILE * TILE,
            bytes_accessed=4 * entries * (own + half) * TILE + 16 * blocks * TILE * TILE,
            transcendentals=0,
        ),
        compiler_params=pltpu.CompilerParams(vmem_limit_bytes=32 << 20),
        name="levels",
    )(depth_id, lat_id, *waves, pool, remote_own, remote_half)
    spread = spread.reshape(levels * lat_size * freq_size, rows, LANES)
    parts = lax.all_to_all(spread, ("depth", "lat", "freq"), 0, 0, tiled=True)
    summed = jnp.sum(parts, axis=0).reshape(1, lateral_width)
    kept = 1.0 - refl
    factor = jnp.where(depth_index == levels - 1, kept * kept, 1.0)
    return summed * factor / (freqs_here * freq_size * shot_total)


def fits_fast(mesh, surface, pool, tile_ids):
    depth, lat, freq = (mesh.shape[name] for name in ("depth", "lat", "freq"))
    freqs, _, shots, width = surface.shape
    rows, slots = tile_ids.shape[1:]
    return (
        depth == 2
        and pool.shape[0] == depth
        and freqs == 3 * freq
        and shots == PACKED * lat
        and TILE == LANES
        and rows * TILE == width
        and rows == SUBLANES * lat
        and 2 * slots < HALF
        and max(rows, pool.shape[2]) <= 256
    )


def solution(mesh):
    placed = (
        P("freq", None, None, "lat"),
        P("depth", "lat"),
        P("depth", "freq", None, None, None),
        P("depth", "lat", None),
        P("depth", "lat", None),
        P("depth", "lat"),
    )

    def whole(surface, refl, pool, tile_ids, block_ids, counts):
        fast = fits_fast(mesh, surface, pool, tile_ids)
        mapped = jax.shard_map(
            per_device_fast if fast else per_device, mesh=mesh, in_specs=placed,
            out_specs=P("depth", "lat"), check_vma=False,
        )
        return mapped(surface, refl, pool, tile_ids, block_ids, counts)

    return whole
```

profile of v0, /device:TPU:0, one launch (start us, length us, event | category | flops | bytes accessed | tf_op | source)
XLA Modules:
  0.0 80.7 jit_solution(252950511776556332)
XLA Ops:
  0.0 3.0 %tables.1 = (f32[16,128]{1,0:T(8,128)}, bf16[8,128,256]{2,1,0:T(8,128)(2,1)}, bf16[8,128,256]{2,1,0:T(8,128)(2,1)}) custom-call(s32[1]{0:T(128)} %bitcast.depth_ref, bf16[1,3,8,128,256]{4,3,2,1,0:T(8,128)(2,1)} %refs_8_.1, f32[1,1024]{1,0:T(1,128)} %refl_ref.1, s32[1,8,10]{2,1,0:T(8,128)} %tiles_ref.1, s32[1,8,10]{2,1,0:T(8,128)} %blocks_ref.1, ...), custom_call_target="tpu_custom_call" | custom-call | tf_op jit(solution)/shard_map/tables/pallas_call | solution.py:309
  3.1 3.1 %collective-permute-start.8 = (bf16[8,128,256]{2,1,0:T(8,128)(2,1)}, bf16[8,128,256]{2,1,0:T(8,128)(2,1)S(1)}, u32[]{:S(2)}, u32[]{:S(2)}) collective-permute-start(bf16[8,128,256]{2,1,0:T(8,128)(2,1)} %get-tuple-element.23), channel_id=1, source_target_pairs={{0,16},{16,0},{1,17},{17,1},{2,18},{18,2},{3,19},{19,3},{4,20},{20... | collective-permute-start | bytes 1572872 | tf_op jit(solution)/shard_map/ppermute | solution.py:318
  6.1 0.1 collective-permute-start.9
  6.2 1.9 %collective-permute-start = (f32[16,128]{1,0:T(8,128)}, f32[16,128]{1,0:T(8,128)S(1)}, u32[]{:S(2)}, u32[]{:S(2)}) collective-permute-start(f32[16,128]{1,0:T(8,128)} %get-tuple-element.15.mine_ref), channel_id=1, source_target_pairs={{0,16},{16,0},{1,17},{17,1},{2,18},{18,2},{3,19},{19,3},{4,20},{20... | collective-permute-start | bytes 24584 | tf_op jit(solution)/shard_map/ppermute | solution.py:317
  8.1 21.5 %collective-permute-done.other_ref = f32[16,128]{1,0:T(8,128)S(1)} collective-permute-done((f32[16,128]{1,0:T(8,128)}, f32[16,128]{1,0:T(8,128)S(1)}, u32[]{:S(2)}, u32[]{:S(2)}) %collective-permute-start) | collective-permute-done | bytes 8224 | tf_op jit(solution)/shard_map/ppermute | solution.py:317
  29.7 0.6 copy-done.2
  30.2 3.0 %front.1 = (bf16[408,128]{1,0:T(8,128)(2,1)}, bf16[408,128]{1,0:T(8,128)(2,1)}, bf16[408,128]{1,0:T(8,128)(2,1)}, bf16[408,128]{1,0:T(8,128)(2,1)}, bf16[408,128...) custom-call(s32[1]{0:T(128)} %bitcast.depth_ref, s32[1]{0:T(128)} %bitcast.1.lat_ref, ...), custom_call_target="tpu_custom_call" | custom-call | tf_op jit(solution)/shard_map/front/pallas_call | solution.py:327
  33.3 1.9 %collective-permute-start.2 = (bf16[408,128]{1,0:T(8,128)(2,1)}, bf16[408,128]{1,0:T(8,128)(2,1)S(1)}, u32[]{:S(2)}, u32[]{:S(2)}) collective-permute-start(bf16[408,128]{1,0:T(8,128)(2,1)} %get-tuple-element.17), channel_id=1, source_target_pairs={{0,4},{2,6},{4,8},{6,10},{8,12},{10,14},{12,0},{14,2},{1,5},{3,7},... | collective-permute-start | bytes 313352 | tf_op jit(solution)/shard_map/ppermute | solution.py:351
  35.1 0.8 %constant_dynamic-slice_fusion.1 = bf16[1,2,2,64,128]{4,3,2,1,0:T(8,128)(2,1)S(1)} fusion(bf16[3,2,16,64,128]{4,3,2,1,0:T(8,128)(2,1)} %bitcast.12, s32[]{:T(128)S(6)} %select_n.17, s32[]{:T(128)S(6)} %select_n.18), kind=kLoop, calls=%fused_computation.5 | loop fusion | bytes 131080 | tf_op jit(solution)/shard_map/dynamic_slice | solution.py:335
  36.0 2.5 %collective-permute-start.3 = (bf16[408,128]{1,0:T(8,128)(2,1)}, bf16[408,128]{1,0:T(8,128)(2,1)S(1)}, u32[]{:S(2)}, u32[]{:S(2)}) collective-permute-start(bf16[408,128]{1,0:T(8,128)(2,1)} %get-tuple-element.18), channel_id=1, source_target_pairs={{0,6},{2,8},{4,10},{6,12},{8,14},{10,0},{12,2},{14,4},{1,7},{3,9},... | collective-permute-start | bytes 313352 | tf_op jit(solution)/shard_map/ppermute | solution.py:351
  38.5 1.2 %collective-permute-start.4 = (bf16[408,128]{1,0:T(8,128)(2,1)}, bf16[408,128]{1,0:T(8,128)(2,1)S(1)}, u32[]{:S(2)}, u32[]{:S(2)}) collective-permute-start(bf16[408,128]{1,0:T(8,128)(2,1)} %get-tuple-element.19), channel_id=1, source_target_pairs={{0,8},{2,10},{4,12},{6,14},{8,0},{10,2},{12,4},{14,6},{1,9},{3,11}... | collective-permute-start | bytes 313352 | tf_op jit(solution)/shard_map/ppermute | solution.py:351
  39.7 0.3 collective-permute-done.2.refs_2_
  40.0 8.7 %collective-permute-start.5 = (bf16[408,128]{1,0:T(8,128)(2,1)}, bf16[408,128]{1,0:T(8,128)(2,1)S(1)}, u32[]{:S(2)}, u32[]{:S(2)}) collective-permute-start(bf16[408,128]{1,0:T(8,128)(2,1)} %get-tuple-element.20), channel_id=1, source_target_pairs={{0,10},{2,12},{4,14},{6,0},{8,2},{10,4},{12,6},{14,8},{1,11},{3,13... | collective-permute-start | bytes 313352 | tf_op jit(solution)/shard_map/ppermute | solution.py:351
  48.8 0.8 constant_dynamic-slice_fusion
  49.5 0.7 slice.3
  50.2 0.0 collective-permute-done.3.refs_3_
  50.2 0.0 collective-permute-start.1
  50.2 0.0 collective-permute-done.4.refs_4_
  50.2 2.7 %collective-permute-start.6 = (bf16[408,128]{1,0:T(8,128)(2,1)}, bf16[408,128]{1,0:T(8,128)(2,1)S(1)}, u32[]{:S(2)}, u32[]{:S(2)}) collective-permute-start(bf16[408,128]{1,0:T(8,128)(2,1)} %get-tuple-element.21), channel_id=1, source_target_pairs={{0,12},{2,14},{4,0},{6,2},{8,4},{10,6},{12,8},{14,10},{1,13},{3,15... | collective-permute-start | bytes 313352 | tf_op jit(solution)/shard_map/ppermute | solution.py:351
  52.9 0.0 collective-permute-done.5.refs_5_
  52.9 2.9 %collective-permute-start.7 = (bf16[408,128]{1,0:T(8,128)(2,1)}, bf16[408,128]{1,0:T(8,128)(2,1)S(1)}, u32[]{:S(2)}, u32[]{:S(2)}) collective-permute-start(bf16[408,128]{1,0:T(8,128)(2,1)} %get-tuple-element.22), channel_id=1, source_target_pairs={{0,14},{2,0},{4,2},{6,4},{8,6},{10,8},{12,10},{14,12},{1,15},{3,1}... | collective-permute-start | bytes 313352 | tf_op jit(solution)/shard_map/ppermute | solution.py:351
  55.9 0.0 copy-start.1
  55.9 0.0 collective-permute-done.6.refs_6_
  55.9 3.1 %collective-permute-done.7.refs_7_ = bf16[408,128]{1,0:T(8,128)(2,1)S(1)} collective-permute-done((bf16[408,128]{1,0:T(8,128)(2,1)}, bf16[408,128]{1,0:T(8,128)(2,1)S(1)}, u32[]{:S(2)}, u32[]{:S(2)}) %collective-permute-start.7) | collective-permute-done | bytes 104480 | tf_op jit(solution)/shard_map/ppermute | solution.py:351
  59.0 0.0 collective-permute-done.1.refs_1_
  59.0 0.0 collective-permute-done.8.refs_9_
  59.0 0.0 collective-permute-done.9.refs_10_
  59.0 0.0 copy-done
  59.1 7.0 %levels.1 = f32[2,8,2,8,128]{4,3,2,1,0:T(8,128)} custom-call(s32[1]{0:T(128)} %bitcast.depth_ref, s32[1]{0:T(128)} %bitcast.1.lat_ref, bf16[408,128]{1,0:T(8,128)(2,1)S(1)} %pad_maximum_fusion.refs_0_, bf16[408,128]{1,0:T(8,128)(2,1)S(1)} %collective-permute-done.1.refs_1_, bf16[408,128]{1,0:T(8,128)(2,1)S(1)} %collective-permute-done.2.refs_2_, ...), custom_call_target="tpu_custom_call" | custom-call | flops 3221225472 | bytes 2883584 | tf_op jit(solution)/shard_map/levels/pallas_call | solution.py:353
  66.0 5.8 %all-to-all-start = ((f32[32,8,128]{2,1,0:T(8,128)}), f32[32,8,128]{2,1,0:T(8,128)S(1)}, u32[]{:S(2)}, u32[]{:S(2)}) async-start(f32[32,8,128]{2,1,0:T(8,128)} %bitcast.9), calls=%async_computation | async-start | bytes 262144 | tf_op jit(solution)/shard_map/all_to_all | solution.py:378
  71.8 8.2 %all-to-all-done = f32[32,8,128]{2,1,0:T(8,128)S(1)} async-done(((f32[32,8,128]{2,1,0:T(8,128)}), f32[32,8,128]{2,1,0:T(8,128)S(1)}, u32[]{:S(2)}, u32[]{:S(2)}) %all-to-all-start) | async-done | bytes 131104 | tf_op jit(solution)/shard_map/all_to_all | solution.py:378
  80.0 0.6 fusion.1
  (5 shorter events, 0.0 us)
Async XLA Ops:
  0.0 59.0 %copy-start = (bf16[1,3,8,128,256]{4,3,2,1,0:T(8,128)(2,1)S(1)}, bf16[1,3,8,128,256]{4,3,2,1,0:T(8,128)(2,1)}, u32[]{:S(2)}) copy-start(bf16[1,3,8,128,256]{4,3,2,1,0:T(8,128)(2,1)} %refs_8_.1) | copy-start | bytes 4718596
  3.1 56.0 %collective-permute-start.8 = (bf16[8,128,256]{2,1,0:T(8,128)(2,1)}, bf16[8,128,256]{2,1,0:T(8,128)(2,1)S(1)}, u32[]{:S(2)}, u32[]{:S(2)}) collective-permute-start(bf16[8,128,256]{2,1,0:T(8,128)(2,1)} %get-tuple-element.23), channel_id=1, source_target_pairs={{0,16},{16,0},{1,17},{17,1},{2,18},{18,2},{3,19},{19,3},{4,20},{20... | collective-permute-start | bytes 1572872 | tf_op jit(solution)/shard_map/ppermute | solution.py:318
  6.1 52.9 %collective-permute-start.9 = (bf16[8,128,256]{2,1,0:T(8,128)(2,1)}, bf16[8,128,256]{2,1,0:T(8,128)(2,1)S(1)}, u32[]{:S(2)}, u32[]{:S(2)}) collective-permute-start(bf16[8,128,256]{2,1,0:T(8,128)(2,1)} %get-tuple-element.24), channel_id=1, source_target_pairs={{0,16},{16,0},{1,17},{17,1},{2,18},{18,2},{3,19},{19,3},{4,20},{20... | collective-permute-start | bytes 1572872 | tf_op jit(solution)/shard_map/ppermute | solution.py:319
  6.2 23.5 %collective-permute-start = (f32[16,128]{1,0:T(8,128)}, f32[16,128]{1,0:T(8,128)S(1)}, u32[]{:S(2)}, u32[]{:S(2)}) collective-permute-start(f32[16,128]{1,0:T(8,128)} %get-tuple-element.15.mine_ref), channel_id=1, source_target_pairs={{0,16},{16,0},{1,17},{17,1},{2,18},{18,2},{3,19},{19,3},{4,20},{20... | collective-permute-start | bytes 24584 | tf_op jit(solution)/shard_map/ppermute | solution.py:317
  29.7 0.6 copy-start.2
  33.3 6.7 %collective-permute-start.2 = (bf16[408,128]{1,0:T(8,128)(2,1)}, bf16[408,128]{1,0:T(8,128)(2,1)S(1)}, u32[]{:S(2)}, u32[]{:S(2)}) collective-permute-start(bf16[408,128]{1,0:T(8,128)(2,1)} %get-tuple-element.17), channel_id=1, source_target_pairs={{0,4},{2,6},{4,8},{6,10},{8,12},{10,14},{12,0},{14,2},{1,5},{3,7},... | collective-permute-start | bytes 313352 | tf_op jit(solution)/shard_map/ppermute | solution.py:351
  36.0 14.2 %collective-permute-start.3 = (bf16[408,128]{1,0:T(8,128)(2,1)}, bf16[408,128]{1,0:T(8,128)(2,1)S(1)}, u32[]{:S(2)}, u32[]{:S(2)}) collective-permute-start(bf16[408,128]{1,0:T(8,128)(2,1)} %get-tuple-element.18), channel_id=1, source_target_pairs={{0,6},{2,8},{4,10},{6,12},{8,14},{10,0},{12,2},{14,4},{1,7},{3,9},... | collective-permute-start | bytes 313352 | tf_op jit(solution)/shard_map/ppermute | solution.py:351
  38.5 11.7 %collective-permute-start.4 = (bf16[408,128]{1,0:T(8,128)(2,1)}, bf16[408,128]{1,0:T(8,128)(2,1)S(1)}, u32[]{:S(2)}, u32[]{:S(2)}) collective-permute-start(bf16[408,128]{1,0:T(8,128)(2,1)} %get-tuple-element.19), channel_id=1, source_target_pairs={{0,8},{2,10},{4,12},{6,14},{8,0},{10,2},{12,4},{14,6},{1,9},{3,11}... | collective-permute-start | bytes 313352 | tf_op jit(solution)/shard_map/ppermute | solution.py:351
  40.0 12.9 %collective-permute-start.5 = (bf16[408,128]{1,0:T(8,128)(2,1)}, bf16[408,128]{1,0:T(8,128)(2,1)S(1)}, u32[]{:S(2)}, u32[]{:S(2)}) collective-permute-start(bf16[408,128]{1,0:T(8,128)(2,1)} %get-tuple-element.20), channel_id=1, source_target_pairs={{0,10},{2,12},{4,14},{6,0},{8,2},{10,4},{12,6},{14,8},{1,11},{3,13... | collective-permute-start | bytes 313352 | tf_op jit(solution)/shard_map/ppermute | solution.py:351
  50.2 8.8 %collective-permute-start.1 = (bf16[408,128]{1,0:T(8,128)(2,1)}, bf16[408,128]{1,0:T(8,128)(2,1)S(1)}, u32[]{:S(2)}, u32[]{:S(2)}) collective-permute-start(bf16[408,128]{1,0:T(8,128)(2,1)} %get-tuple-element.16), channel_id=1, source_target_pairs={{0,2},{2,4},{4,6},{6,8},{8,10},{10,12},{12,14},{14,0},{1,3},{3,5},... | collective-permute-start | bytes 313352 | tf_op jit(solution)/shard_map/ppermute | solution.py:351
  50.2 5.7 %collective-permute-start.6 = (bf16[408,128]{1,0:T(8,128)(2,1)}, bf16[408,128]{1,0:T(8,128)(2,1)S(1)}, u32[]{:S(2)}, u32[]{:S(2)}) collective-permute-start(bf16[408,128]{1,0:T(8,128)(2,1)} %get-tuple-element.21), channel_id=1, source_target_pairs={{0,12},{2,14},{4,0},{6,2},{8,4},{10,6},{12,8},{14,10},{1,13},{3,15... | collective-permute-start | bytes 313352 | tf_op jit(solution)/shard_map/ppermute | solution.py:351
  52.9 6.1 %collective-permute-start.7 = (bf16[408,128]{1,0:T(8,128)(2,1)}, bf16[408,128]{1,0:T(8,128)(2,1)S(1)}, u32[]{:S(2)}, u32[]{:S(2)}) collective-permute-start(bf16[408,128]{1,0:T(8,128)(2,1)} %get-tuple-element.22), channel_id=1, source_target_pairs={{0,14},{2,0},{4,2},{6,4},{8,6},{10,8},{12,10},{14,12},{1,15},{3,1}... | collective-permute-start | bytes 313352 | tf_op jit(solution)/shard_map/ppermute | solution.py:351
  55.9 24.2 %copy-start.1 = (f32[1,1024]{1,0:T(1,128)S(1)}, f32[1,1024]{1,0:T(1,128)}, u32[]{:S(2)}) copy-start(f32[1,1024]{1,0:T(1,128)} %refl_ref.1) | copy-start | bytes 12292
  66.0 14.0 %all-to-all-start = ((f32[32,8,128]{2,1,0:T(8,128)}), f32[32,8,128]{2,1,0:T(8,128)S(1)}, u32[]{:S(2)}, u32[]{:S(2)}) async-start(f32[32,8,128]{2,1,0:T(8,128)} %bitcast.9), calls=%async_computation | async-start | bytes 262144 | tf_op jit(solution)/shard_map/all_to_all | solution.py:378
where the time goes:
time: 81.2 us; the launch traced here: 80.7 us
  waiting for transfers between devices  33.2 us (41%)
  starting transfers between devices  30.8 us (38%)
  Pallas kernels  13 us (16%)
  local copies, waits for them, and re-layouts  2.9 us (4%)
    ppermute x1, waiting for transfers between devices, per_device_fast(): other = lax.ppermute(mine, 'depth', swap)  21.5 us
    ppermute x7, starting transfers between devices, per_device_fast(): waves[turn] = lax.ppermute(chunks[turn - 1], 'lat', around)  20 us
    all_to_all x1, waiting for transfers between devices, per_device_fast(): parts = lax.all_to_all(spread, ('depth', 'lat', 'freq'), 0, 0, tiled=True)  8.2 us
    pallas_call x1, Pallas kernels, per_device_fast(): pl.pallas_call(functools.partial(level_kernel, lat_size, freq_size, slots...  6.98 us
    all_to_all x1, starting transfers between devices, per_device_fast(): parts = lax.all_to_all(spread, ('depth', 'lat', 'freq'), 0, 0, tiled=True)  5.76 us
    ppermute x7, waiting for transfers between devices, per_device_fast(): waves[turn] = lax.ppermute(chunks[turn - 1], 'lat', around)  3.45 us
    ppermute x1, starting transfers between devices, per_device_fast(): remote_own = lax.ppermute(send_own, 'depth', swap)  3.06 us
    pallas_call x1, Pallas kernels, per_device_fast(): pl.pallas_call(table_kernel, out_shape=[jax.ShapeDtypeStruct((2 * rows, L...  3.04 us
  transfers between devices with their start and end apart: 11, of which 4 were waited for; matrix products, arithmetic and copies ran while one was open for 3% of the time, Pallas kernels for 4%

commit v1 on v0

--- a/solution.py
+++ b/solution.py
@@ -93,6 +93,7 @@
 
 
 ROWS_STEP = 4
+FAR = 1
 LANES = 128
 SUBLANES = 8
 HALF = LANES // 2
@@ -102,13 +103,36 @@
 ANY_SPACE = pl.BlockSpec(memory_space=pl.ANY)
 
 
-def table_kernel(
-    depth_ref, pool_ref, refl_ref, tiles_ref, blocks_ref, counts_ref, out_ref, own_ref, half_ref, sems
+def chunk_copies(surface_ref, depth_index, target, lat_size, out, sems):
+    groups = surface_ref.shape[2] // lat_size
+    height = surface_ref.shape[3]
+    sources = [
+        surface_ref.at[2 * depth_index, part, groups * target + group]
+        for part in range(2)
+        for group in range(groups)
+    ] + [surface_ref.at[1, part, depth_index * lat_size + target] for part in range(2)]
+    return [
+        pltpu.make_async_copy(source, out.at[pl.ds(place * height, height), :], sems.at[place])
+        for place, source in enumerate(sources)
+    ]
+
+
+def first_kernel(
+    lat_size, turns, depth_ref, lat_ref, surface_ref, pool_ref, refl_ref, tiles_ref, blocks_ref,
+    counts_ref, *refs,
 ):
+    out_ref, own_ref, half_ref = refs[:3]
+    chunks, sems = refs[3:-1], refs[-1]
+    depth_index = depth_ref[0]
     copies = [
-        pltpu.make_async_copy(pool_ref.at[0, 2 * (1 - depth_ref[0])], own_ref, sems.at[0]),
-        pltpu.make_async_copy(pool_ref.at[0, 1], half_ref, sems.at[1]),
+        pltpu.make_async_copy(pool_ref.at[0, 2 * (1 - depth_index)], own_ref, sems.at[len(turns), 0]),
+        pltpu.make_async_copy(pool_ref.at[0, 1], half_ref, sems.at[len(turns), 1]),
     ]
+    for place, turn in enumerate(turns):
+        target = lax.rem(lat_ref[0] + turn, lat_size)
+        copies += chunk_copies(
+            surface_ref, depth_index, target, lat_size, chunks[place], sems.at[place]
+        )
     for copy in copies:
         copy.start()
     rows = tiles_ref.shape[1]
@@ -127,47 +151,36 @@
         copy.wait()
 
 
-def front_kernel(lat_size, depth_ref, lat_ref, surface_ref, mine_ref, other_ref, *refs):
-    outs, sems = refs[:-1], refs[-1]
+def second_kernel(lat_size, turns, depth_ref, lat_ref, surface_ref, mine_ref, other_ref, *refs):
+    chunks, lists_ref, sems = refs[:-2], refs[-2], refs[-1]
     depth_index = depth_ref[0]
-    groups = surface_ref.shape[2] // lat_size
-    height = surface_ref.shape[3]
-    rows = height // SUBLANES
+    rows = mine_ref.shape[0] // 2
     copies = []
-    for turn, out in enumerate(outs, 1):
+    for place, turn in enumerate(turns):
         target = lax.rem(lat_ref[0] + turn, lat_size)
-        sources = [
-            surface_ref.at[2 * depth_index, part, groups * target + group]
-            for part in range(2)
-            for group in range(groups)
-        ] + [surface_ref.at[1, part, depth_index * lat_size + target] for part in range(2)]
-        copies += [
-            pltpu.make_async_copy(
-                source, out.at[pl.ds(place * height, height), :], sems.at[turn - 1, place]
-            )
-            for place, source in enumerate(sources)
-        ]
+        copies += chunk_copies(
+            surface_ref, depth_index, target, lat_size, chunks[place], sems.at[place]
+        )
     for copy in copies:
         copy.start()
     first = jnp.where(depth_index == 0, mine_ref[...], other_ref[...])
     second = jnp.where(depth_index == 0, other_ref[rows:, :], mine_ref[rows:, :])
     refl = first[:rows]
-    high = refl.astype(jnp.bfloat16)
-    low = (refl - high.astype(jnp.float32)).astype(jnp.bfloat16)
-    lists = first[rows:] + pltpu.roll(second, HALF, 1)
-    pair = jnp.concatenate([high.astype(jnp.float32), low.astype(jnp.float32)], axis=0)
-    for out in outs:
+    high = refl.astype(jnp.bfloat16).astype(jnp.float32)
+    pair = jnp.concatenate([high, refl - high], axis=0).astype(jnp.bfloat16)
+    lists = (first[rows:] + pltpu.roll(second, HALF, 1)).astype(jnp.bfloat16)
+    for out in [*chunks, lists_ref]:
         start = out.shape[0] - 3 * rows
-        out[start:start + 2 * rows, :] = pair.astype(jnp.bfloat16)
-        out[start + 2 * rows:, :] = lists.astype(jnp.bfloat16)
+        out[start:start + 2 * rows, :] = pair
+        out[start + 2 * rows:, :] = lists
     for copy in copies:
         copy.wait()
 
 
 def level_kernel(lat_size, freq_size, slots, levels, depth_ref, lat_ref, *refs):
-    wave_refs = refs[:lat_size]
+    wave_refs, tail_refs, refs = refs[:lat_size], refs[lat_size:2 * lat_size], refs[2 * lat_size:]
     (local_ref, remote_own_ref, remote_half_ref, image_ref, table, own_buf, half_buf, squares_buf,
-     lists_buf, factor_buf, index_buf, index_ref, sem) = refs[lat_size:]
+     lists_buf, factor_buf, index_buf, index_ref, sem) = refs
     blocks = remote_own_ref.shape[0]
     entries = factor_buf.shape[1]
     rows = entries // lat_size
@@ -175,12 +188,12 @@
     half = own // 2
     unit = 2 * (own + half)
     depth_index = depth_ref[0]
-    for turn, wave in enumerate(wave_refs):
+    for turn, tail in enumerate(tail_refs):
         source = lax.rem(lat_ref[0] + lat_size - turn, lat_size)
-        top = wave.shape[0] - 3 * rows
-        pair = wave[top:top + 2 * rows, :].astype(jnp.float32)
+        top = tail.shape[0] - 3 * rows
+        pair = tail[top:top + 2 * rows, :].astype(jnp.float32)
         high, low = pair[:rows], pair[rows:]
-        lists = wave[top + 2 * rows:, :].astype(jnp.float32)
+        lists = tail[top + 2 * rows:, :].astype(jnp.float32)
         start = pl.multiple_of(source * rows, rows)
         factor_buf[0, pl.ds(start, rows), :] = 1.0 - (high + low)
         lists_buf[pl.ds(start, rows), :] = lists
@@ -289,6 +302,11 @@
                 image_ref[level, target, copy] = summed[start:start + rows]
 
 
+def turns_of(lat_size):
+    turns = sorted(range(1, lat_size), key=lambda turn: abs(turn - lat_size // 2))
+    return turns[:FAR], turns[FAR:]
+
+
 def per_device_fast(surface, refl, pool, tile_ids, block_ids, counts):
     depth_index = lax.axis_index("depth")
     lat_index = lax.axis_index("lat")
@@ -305,55 +323,60 @@
     depth_id = depth_index.astype(jnp.int32).reshape(1)
     lat_id = lat_index.astype(jnp.int32).reshape(1)
 
-    sent = jax.ShapeDtypeStruct(pool.shape[2:], pool.dtype)
-    mine, send_own, send_half = pl.pallas_call(
-        table_kernel,
-        out_shape=[jax.ShapeDtypeStruct((2 * rows, LANES), jnp.float32), sent, sent],
-        in_specs=[SMEM_SPACE, ANY_SPACE] + [VMEM_SPACE] * 4,
-        out_specs=[VMEM_SPACE] * 3,
-        scratch_shapes=[pltpu.SemaphoreType.DMA((2,))],
-        name="tables",
-    )(depth_id, pool, refl, tile_ids, block_ids, counts)
-    other = lax.ppermute(mine, "depth", swap)
-    remote_own = lax.ppermute(send_own, "depth", swap)
-    remote_half = lax.ppermute(send_half, "depth", swap)
-
     pieces = surface.reshape(
         freqs_here, 2, shot_total // SUBLANES, SUBLANES, rows, LANES
     ).transpose(0, 1, 2, 4, 3, 5).reshape(
         freqs_here, 2, shot_total // SUBLANES, rows * SUBLANES, LANES
     )
-    height = (2 * (own + half) + 3) * rows
-    chunks = pl.pallas_call(
-        functools.partial(front_kernel, lat_size),
-        out_shape=[jax.ShapeDtypeStruct((height, LANES), jnp.bfloat16)] * (lat_size - 1),
+    cuts = 2 * (own + half) // SUBLANES
+    height = cuts * rows * SUBLANES
+    tail = 3 * rows
+    far, near = turns_of(lat_size)
+
+    def bf16_out(length):
+        return jax.ShapeDtypeStruct((length, LANES), jnp.bfloat16)
+
+    sent = jax.ShapeDtypeStruct(pool.shape[2:], pool.dtype)
+    mine, send_own, send_half, *far_chunks = pl.pallas_call(
+        functools.partial(first_kernel, lat_size, far),
+        out_shape=[jax.ShapeDtypeStruct((2 * rows, LANES), jnp.float32), sent, sent]
+        + [bf16_out(height)] * len(far),
+        in_specs=[SMEM_SPACE] * 2 + [ANY_SPACE] * 2 + [VMEM_SPACE] * 4,
+        out_specs=[VMEM_SPACE] * (3 + len(far)),
+        scratch_shapes=[pltpu.SemaphoreType.DMA((len(far) + 1, cuts))],
+        name="first",
+    )(depth_id, lat_id, pieces, pool, refl, tile_ids, block_ids, counts)
+    other = lax.ppermute(mine, "depth", swap)
+    remote_own = lax.ppermute(send_own, "depth", swap)
+    remote_half = lax.ppermute(send_half, "depth", swap)
+    waves, tails = {}, {}
+
+    def around(turn):
+        return [(source, (source + turn) % lat_size) for source in range(lat_size)]
+
+    for turn, chunk in zip(far, far_chunks):
+        waves[turn] = lax.ppermute(chunk, "lat", around(turn))
+    *near_chunks, stay, lists = pl.pallas_call(
+        functools.partial(second_kernel, lat_size, near + [0]),
+        out_shape=[bf16_out(height + tail)] * (len(near) + 1) + [bf16_out(tail)],
         in_specs=[SMEM_SPACE] * 2 + [ANY_SPACE] + [VMEM_SPACE] * 2,
-        out_specs=[VMEM_SPACE] * (lat_size - 1),
-        scratch_shapes=[pltpu.SemaphoreType.DMA((lat_size - 1, 2 * (own + half) // SUBLANES))],
-        name="front",
+        out_specs=[VMEM_SPACE] * (len(near) + 2),
+        scratch_shapes=[pltpu.SemaphoreType.DMA((len(near) + 1, cuts))],
+        compiler_params=pltpu.CompilerParams(vmem_limit_bytes=8 << 20),
+        name="second",
     )(depth_id, lat_id, pieces, mine, other)
-    own_pieces = lax.dynamic_slice(
-        pieces, (2 * depth_index, 0, lat_index * (own // SUBLANES), 0, 0),
-        (1, 2, own // SUBLANES, rows * SUBLANES, LANES),
-    )
-    half_pieces = lax.dynamic_slice(
-        pieces, (1, 0, depth_index * lat_size + lat_index, 0, 0), (1, 2, 1, rows * SUBLANES, LANES)
-    )
-    stay = jnp.concatenate(
-        [part.reshape(-1, LANES) for part in (own_pieces, half_pieces)]
-        + [chunks[0][height - 3 * rows:]], axis=0,
-    )
-    middle = lat_size // 2
-    order = sorted(range(1, lat_size), key=lambda turn: abs(turn - middle))
-    waves = [stay] + [None] * (lat_size - 1)
-    for turn in order:
-        around = [(source, (source + turn) % lat_size) for source in range(lat_size)]
-        waves[turn] = lax.ppermute(chunks[turn - 1], "lat", around)
+    for turn, chunk in zip(near, near_chunks):
+        tails[turn] = waves[turn] = lax.ppermute(chunk, "lat", around(turn))
+    for turn in far:
+        tails[turn] = lax.ppermute(lists, "lat", around(turn))
+    waves[0] = tails[0] = stay
+    waves = [waves[turn] for turn in range(lat_size)]
+    tails = [tails[turn] for turn in range(lat_size)]
 
     spread = pl.pallas_call(
         functools.partial(level_kernel, lat_size, freq_size, slots, levels),
         out_shape=jax.ShapeDtypeStruct((levels, lat_size, freq_size, rows, LANES), jnp.float32),
-        in_specs=[SMEM_SPACE] * 2 + [VMEM_SPACE] * (lat_size + 3),
+        in_specs=[SMEM_SPACE] * 2 + [VMEM_SPACE] * (2 * lat_size + 3),
         out_specs=VMEM_SPACE,
         scratch_shapes=[
             pltpu.VMEM(((blocks * entries + 1) * 2 * (own + half), LANES), jnp.float32),
@@ -373,7 +396,7 @@
         ),
         compiler_params=pltpu.CompilerParams(vmem_limit_bytes=32 << 20),
         name="levels",
-    )(depth_id, lat_id, *waves, pool, remote_own, remote_half)
+    )(depth_id, lat_id, *waves, *tails, pool, remote_own, remote_half)
     spread = spread.reshape(levels * lat_size * freq_size, rows, LANES)
     parts = lax.all_to_all(spread, ("depth", "lat", "freq"), 0, 0, tiled=True)
     summed = jnp.sum(parts, axis=0).reshape(1, lateral_width)

time: 81.2 us -> 76.9 us (0.947)
  starting transfers between devices: 30.8 us -> 27.9 us
  waiting for transfers between devices: 33.2 us -> 35.6 us
  local copies, waits for them, and re-layouts: 2.9 us -> 0.71 us
  Pallas kernels: 13 us -> 11.7 us
    ppermute x7 -> x8, waiting for transfers between devices: 3.45 us -> 8.52 us  [the longest x6 8.29 us: per_device_fast(): tails[turn] = waves[turn] = lax.ppermute(chunk, 'lat', around(turn))]
    ppermute x7 -> x8, starting transfers between devices: 20 us -> 16.8 us  [the longest x6 10.9 us: per_device_fast(): tails[turn] = waves[turn] = lax.ppermute(chunk, 'lat', around(turn))]
    ppermute x1, waiting for transfers between devices: 21.5 us -> 18.9 us  [per_device_fast(): other = lax.ppermute(mine, 'depth', swap)]
    dynamic_slice x2 -> x0, local copies, waits for them, and re-layouts: 1.61 us -> none  [the longest x1 0.84 us: per_device_fast(): lax.dynamic_slice(pieces, (2 * depth_index, 0, lat_index * (own // SUBLAN...]
    pallas_call x2, Pallas kernels: 6.07 us -> 4.63 us  [the longest x1 3.19 us: per_device_fast(): pl.pallas_call(functools.partial(first_kernel, lat_size, far), out_shape=...]
  transfers between devices with their start and end apart: 11 -> 12, of which waited for: 4 -> 7; matrix products, arithmetic and copies ran while one was open for 3% -> 0% of each run, Pallas kernels for 4% -> 2%
where the time goes in v1:
time: 76.9 us; the launch traced here: 76.6 us
  waiting for transfers between devices  35.6 us (46%)
  starting transfers between devices  27.9 us (36%)
  Pallas kernels  11.7 us (15%)
    ppermute x1, waiting for transfers between devices, per_device_fast(): other = lax.ppermute(mine, 'depth', swap)  18.9 us
    ppermute x6, starting transfers between devices, per_device_fast(): tails[turn] = waves[turn] = lax.ppermute(chunk, 'lat', around(turn))  10.9 us
    ppermute x6, waiting for transfers between devices, per_device_fast(): tails[turn] = waves[turn] = lax.ppermute(chunk, 'lat', around(turn))  8.29 us
    all_to_all x1, waiting for transfers between devices, per_device_fast(): parts = lax.all_to_all(spread, ('depth', 'lat', 'freq'), 0, 0, tiled=True)  8.2 us
    pallas_call x1, Pallas kernels, per_device_fast(): pl.pallas_call(functools.partial(level_kernel, lat_size, freq_size, slots...  7.05 us
    all_to_all x1, starting transfers between devices, per_device_fast(): parts = lax.all_to_all(spread, ('depth', 'lat', 'freq'), 0, 0, tiled=True)  6.45 us
    pallas_call x1, Pallas kernels, per_device_fast(): pl.pallas_call(functools.partial(first_kernel, lat_size, far), out_shape=...  3.19 us
    ppermute x1, starting transfers between devices, per_device_fast(): remote_own = lax.ppermute(send_own, 'depth', swap)  3.06 us
  transfers between devices with their start and end apart: 12, of which 7 were waited for; matrix products, arithmetic and copies ran while one was open for 0% of the time, Pallas kernels for 2%

profile of v1, /device:TPU:0, one launch (start us, length us, event | category | flops | bytes accessed | tf_op | source)
XLA Modules:
  0.0 76.6 jit_solution(5344587379948575340)
XLA Ops:
  0.0 3.2 %first.1 = (f32[16,128]{1,0:T(8,128)}, bf16[8,128,256]{2,1,0:T(8,128)(2,1)}, bf16[8,128,256]{2,1,0:T(8,128)(2,1)}, bf16[384,128]{1,0:T(8,128)(2,1)}) custom-call(s32[1]{0:T(128)} %bitcast.depth_ref, s32[1]{0:T(128)} %bitcast.1.lat_ref, bf16[3,2,16,64,128]{4,3,2,1,0:T(8,128)(2,1)} %bitcast.9, bf16[1,3,8,128,256]{4,3,2,1,0:T(8,128)(2,1)} %refs_16_.1, ...), custom_call_target="tpu_custom_call" | custom-call | tf_op jit(solution)/shard_map/first/pallas_call | solution.py:340
  3.2 0.0 copy-start.1
  3.2 3.1 %collective-permute-start.9 = (bf16[8,128,256]{2,1,0:T(8,128)(2,1)}, bf16[8,128,256]{2,1,0:T(8,128)(2,1)S(1)}, u32[]{:S(2)}, u32[]{:S(2)}) collective-permute-start(bf16[8,128,256]{2,1,0:T(8,128)(2,1)} %get-tuple-element.27), channel_id=1, source_target_pairs={{0,16},{16,0},{1,17},{17,1},{2,18},{18,2},{3,19},{19,3},{4,20},{20... | collective-permute-start | bytes 1572872 | tf_op jit(solution)/shard_map/ppermute | solution.py:350
  6.3 0.1 collective-permute-start.10
  6.4 3.0 %collective-permute-start.4 = (bf16[384,128]{1,0:T(8,128)(2,1)}, bf16[384,128]{1,0:T(8,128)(2,1)S(1)}, u32[]{:S(2)}, u32[]{:S(2)}) collective-permute-start(bf16[384,128]{1,0:T(8,128)(2,1)} %get-tuple-element.22), channel_id=1, source_target_pairs={{0,8},{2,10},{4,12},{6,14},{8,0},{10,2},{12,4},{14,6},{1,9},{3,11}... | collective-permute-start | bytes 294920 | tf_op jit(solution)/shard_map/ppermute | solution.py:358
  9.4 1.5 %collective-permute-start = (f32[16,128]{1,0:T(8,128)}, f32[16,128]{1,0:T(8,128)S(1)}, u32[]{:S(2)}, u32[]{:S(2)}) collective-permute-start(f32[16,128]{1,0:T(8,128)} %get-tuple-element.17.mine_ref), channel_id=1, source_target_pairs={{0,16},{16,0},{1,17},{17,1},{2,18},{18,2},{3,19},{19,3},{4,20},{20... | collective-permute-start | bytes 24584 | tf_op jit(solution)/shard_map/ppermute | solution.py:349
  10.9 18.9 %collective-permute-done.other_ref = f32[16,128]{1,0:T(8,128)S(1)} collective-permute-done((f32[16,128]{1,0:T(8,128)}, f32[16,128]{1,0:T(8,128)S(1)}, u32[]{:S(2)}, u32[]{:S(2)}) %collective-permute-start) | collective-permute-done | bytes 8224 | tf_op jit(solution)/shard_map/ppermute | solution.py:349
  29.8 0.7 copy-done.2
  30.5 1.4 %second.1 = (bf16[408,128]{1,0:T(8,128)(2,1)S(1)}, bf16[408,128]{1,0:T(8,128)(2,1)S(1)}, bf16[408,128]{1,0:T(8,128)(2,1)S(1)}, bf16[408,128]{1,0:T(8,128)(2,1)S(...) custom-call(s32[1]{0:T(128)} %bitcast.depth_ref, ...), custom_call_target="tpu_custom_call" | custom-call | tf_op jit(solution)/shard_map/second/pallas_call | solution.py:359
  32.0 2.9 %collective-permute-start.8 = (bf16[24,128]{1,0:T(8,128)(2,1)S(1)}, bf16[24,128]{1,0:T(8,128)(2,1)S(1)}, u32[]{:S(2)}, u32[]{:S(2)}) collective-permute-start(bf16[24,128]{1,0:T(8,128)(2,1)S(1)} %get-tuple-element.26), channel_id=1, source_target_pairs={{0,8},{2,10},{4,12},{6,14},{8,0},{10,2},{12,4},{14,6},{1,9},{3,11}... | collective-permute-start | bytes 18440 | tf_op jit(solution)/shard_map/ppermute | solution.py:371
  34.8 1.5 %collective-permute-start.1 = (bf16[408,128]{1,0:T(8,128)(2,1)S(1)}, bf16[408,128]{1,0:T(8,128)(2,1)S(1)}, u32[]{:S(2)}, u32[]{:S(2)}) collective-permute-start(bf16[408,128]{1,0:T(8,128)(2,1)S(1)} %get-tuple-element.19), channel_id=1, source_target_pairs={{0,2},{2,4},{4,6},{6,8},{8,10},{10,12},{12,14},{14,0},{1,3},{3,5},... | collective-permute-start | bytes 313352 | tf_op jit(solution)/shard_map/ppermute | solution.py:369
  36.3 0.2 collective-permute-done.8.refs_12_
  36.6 1.8 %collective-permute-start.2 = (bf16[408,128]{1,0:T(8,128)(2,1)S(1)}, bf16[408,128]{1,0:T(8,128)(2,1)S(1)}, u32[]{:S(2)}, u32[]{:S(2)}) collective-permute-start(bf16[408,128]{1,0:T(8,128)(2,1)S(1)} %get-tuple-element.20), channel_id=1, source_target_pairs={{0,4},{2,6},{4,8},{6,10},{8,12},{10,14},{12,0},{14,2},{1,5},{3,7},... | collective-permute-start | bytes 313352 | tf_op jit(solution)/shard_map/ppermute | solution.py:369
  38.4 0.0 collective-permute-done.4.refs_4_
  38.4 2.6 %collective-permute-start.3 = (bf16[408,128]{1,0:T(8,128)(2,1)S(1)}, bf16[408,128]{1,0:T(8,128)(2,1)S(1)}, u32[]{:S(2)}, u32[]{:S(2)}) collective-permute-start(bf16[408,128]{1,0:T(8,128)(2,1)S(1)} %get-tuple-element.21), channel_id=1, source_target_pairs={{0,6},{2,8},{4,10},{6,12},{8,14},{10,0},{12,2},{14,4},{1,7},{3,9},... | collective-permute-start | bytes 313352 | tf_op jit(solution)/shard_map/ppermute | solution.py:369
  40.9 2.5 %collective-permute-done.1.refs_1_.refs_9_ = bf16[408,128]{1,0:T(8,128)(2,1)S(1)} collective-permute-done((bf16[408,128]{1,0:T(8,128)(2,1)S(1)}, bf16[408,128]{1,0:T(8,128)(2,1)S(1)}, u32[]{:S(2)}, u32[]{:S(2)}) %collective-permute-start.1) | collective-permute-done | bytes 104480 | tf_op jit(solution)/shard_map/ppermute | solution.py:369
  43.4 0.0 collective-permute-start.5
  43.4 0.8 %collective-permute-done.2.refs_2_.refs_10_ = bf16[408,128]{1,0:T(8,128)(2,1)S(1)} collective-permute-done((bf16[408,128]{1,0:T(8,128)(2,1)S(1)}, bf16[408,128]{1,0:T(8,128)(2,1)S(1)}, u32[]{:S(2)}, u32[]{:S(2)}) %collective-permute-start.2) | collective-permute-done | bytes 104480 | tf_op jit(solution)/shard_map/ppermute | solution.py:369
  44.3 1.2 %collective-permute-start.6 = (bf16[408,128]{1,0:T(8,128)(2,1)S(1)}, bf16[408,128]{1,0:T(8,128)(2,1)S(1)}, u32[]{:S(2)}, u32[]{:S(2)}) collective-permute-start(bf16[408,128]{1,0:T(8,128)(2,1)S(1)} %get-tuple-element.24), channel_id=1, source_target_pairs={{0,12},{2,14},{4,0},{6,2},{8,4},{10,6},{12,8},{14,10},{1,13},{3,15... | collective-permute-start | bytes 313352 | tf_op jit(solution)/shard_map/ppermute | solution.py:369
  45.4 2.7 %collective-permute-done.3.refs_3_.refs_11_ = bf16[408,128]{1,0:T(8,128)(2,1)S(1)} collective-permute-done((bf16[408,128]{1,0:T(8,128)(2,1)S(1)}, bf16[408,128]{1,0:T(8,128)(2,1)S(1)}, u32[]{:S(2)}, u32[]{:S(2)}) %collective-permute-start.3) | collective-permute-done | bytes 104480 | tf_op jit(solution)/shard_map/ppermute | solution.py:369
  48.1 3.9 %collective-permute-start.7 = (bf16[408,128]{1,0:T(8,128)(2,1)S(1)}, bf16[408,128]{1,0:T(8,128)(2,1)S(1)}, u32[]{:S(2)}, u32[]{:S(2)}) collective-permute-start(bf16[408,128]{1,0:T(8,128)(2,1)S(1)} %get-tuple-element.25), channel_id=1, source_target_pairs={{0,14},{2,0},{4,2},{6,4},{8,6},{10,8},{12,10},{14,12},{1,15},{3,1}... | collective-permute-start | bytes 313352 | tf_op jit(solution)/shard_map/ppermute | solution.py:369
  52.0 0.0 collective-permute-done.5.refs_5_.refs_13_
  52.0 0.0 collective-permute-done.6.refs_6_.refs_14_
  52.0 2.3 %collective-permute-done.7.refs_7_.refs_15_ = bf16[408,128]{1,0:T(8,128)(2,1)S(1)} collective-permute-done((bf16[408,128]{1,0:T(8,128)(2,1)S(1)}, bf16[408,128]{1,0:T(8,128)(2,1)S(1)}, u32[]{:S(2)}, u32[]{:S(2)}) %collective-permute-start.7) | collective-permute-done | bytes 104480 | tf_op jit(solution)/shard_map/ppermute | solution.py:369
  54.2 0.0 collective-permute-done.9.refs_17_
  54.2 0.0 collective-permute-done.10.refs_18_
  54.2 0.0 copy-start.3
  54.3 7.1 %levels.1 = f32[2,8,2,8,128]{4,3,2,1,0:T(8,128)} custom-call(s32[1]{0:T(128)} %bitcast.depth_ref, s32[1]{0:T(128)} %bitcast.1.lat_ref, bf16[408,128]{1,0:T(8,128)(2,1)S(1)} %get-tuple-element.18.refs_0_.refs_8_, bf16[408,128]{1,0:T(8,128)(2,1)S(1)} %collective-permute-done.1.refs_1_.refs_9_, bf16[408,128]{1,0:T(8,128)(2,1)S(1)} %collective-permute-done.2.refs_2_.refs_10_, ...), custom_call_target="tpu_custom_call" | custom-call | flops 3221225472 | bytes 2883584 | tf_op jit(solution)/shard_map/levels/pallas_call | solution.py:376
  61.3 6.5 %all-to-all-start = ((f32[32,8,128]{2,1,0:T(8,128)}), f32[32,8,128]{2,1,0:T(8,128)S(1)}, u32[]{:S(2)}, u32[]{:S(2)}) async-start(f32[32,8,128]{2,1,0:T(8,128)} %bitcast.7), calls=%async_computation | async-start | bytes 262144 | tf_op jit(solution)/shard_map/all_to_all | solution.py:401
  67.8 8.2 %all-to-all-done = f32[32,8,128]{2,1,0:T(8,128)S(1)} async-done(((f32[32,8,128]{2,1,0:T(8,128)}), f32[32,8,128]{2,1,0:T(8,128)S(1)}, u32[]{:S(2)}, u32[]{:S(2)}) %all-to-all-start) | async-done | bytes 131104 | tf_op jit(solution)/shard_map/all_to_all | solution.py:401
  76.0 0.0 copy-done.3
  76.0 0.6 fusion.1
  (5 shorter events, 0.0 us)
Async XLA Ops:
  0.0 29.8 %copy-start = (bf16[3,2,128,1024]{3,2,1,0:T(8,128)(2,1)S(1)}, bf16[3,2,128,1024]{3,2,1,0:T(8,128)(2,1)}, u32[]{:S(2)}) copy-start(bf16[3,2,128,1024]{3,2,1,0:T(8,128)(2,1)} %param.6) | copy-start | bytes 4718596
  3.2 51.0 %copy-start.1 = (bf16[1,3,8,128,256]{4,3,2,1,0:T(8,128)(2,1)S(1)}, bf16[1,3,8,128,256]{4,3,2,1,0:T(8,128)(2,1)}, u32[]{:S(2)}) copy-start(bf16[1,3,8,128,256]{4,3,2,1,0:T(8,128)(2,1)} %refs_16_.1) | copy-start | bytes 4718596
  3.2 51.0 %collective-permute-start.9 = (bf16[8,128,256]{2,1,0:T(8,128)(2,1)}, bf16[8,128,256]{2,1,0:T(8,128)(2,1)S(1)}, u32[]{:S(2)}, u32[]{:S(2)}) collective-permute-start(bf16[8,128,256]{2,1,0:T(8,128)(2,1)} %get-tuple-element.27), channel_id=1, source_target_pairs={{0,16},{16,0},{1,17},{17,1},{2,18},{18,2},{3,19},{19,3},{4,20},{20... | collective-permute-start | bytes 1572872 | tf_op jit(solution)/shard_map/ppermute | solution.py:350
  6.3 48.0 %collective-permute-start.10 = (bf16[8,128,256]{2,1,0:T(8,128)(2,1)}, bf16[8,128,256]{2,1,0:T(8,128)(2,1)S(1)}, u32[]{:S(2)}, u32[]{:S(2)}) collective-permute-start(bf16[8,128,256]{2,1,0:T(8,128)(2,1)} %get-tuple-element.28), channel_id=1, source_target_pairs={{0,16},{16,0},{1,17},{17,1},{2,18},{18,2},{3,19},{19,3},{4,20},{20... | collective-permute-start | bytes 1572872 | tf_op jit(solution)/shard_map/ppermute | solution.py:351
  6.4 32.0 %collective-permute-start.4 = (bf16[384,128]{1,0:T(8,128)(2,1)}, bf16[384,128]{1,0:T(8,128)(2,1)S(1)}, u32[]{:S(2)}, u32[]{:S(2)}) collective-permute-start(bf16[384,128]{1,0:T(8,128)(2,1)} %get-tuple-element.22), channel_id=1, source_target_pairs={{0,8},{2,10},{4,12},{6,14},{8,0},{10,2},{12,4},{14,6},{1,9},{3,11}... | collective-permute-start | bytes 294920 | tf_op jit(solution)/shard_map/ppermute | solution.py:358
  9.4 20.5 %collective-permute-start = (f32[16,128]{1,0:T(8,128)}, f32[16,128]{1,0:T(8,128)S(1)}, u32[]{:S(2)}, u32[]{:S(2)}) collective-permute-start(f32[16,128]{1,0:T(8,128)} %get-tuple-element.17.mine_ref), channel_id=1, source_target_pairs={{0,16},{16,0},{1,17},{17,1},{2,18},{18,2},{3,19},{19,3},{4,20},{20... | collective-permute-start | bytes 24584 | tf_op jit(solution)/shard_map/ppermute | solution.py:349
  29.8 0.7 copy-start.2
  32.0 4.6 %collective-permute-start.8 = (bf16[24,128]{1,0:T(8,128)(2,1)S(1)}, bf16[24,128]{1,0:T(8,128)(2,1)S(1)}, u32[]{:S(2)}, u32[]{:S(2)}) collective-permute-start(bf16[24,128]{1,0:T(8,128)(2,1)S(1)} %get-tuple-element.26), channel_id=1, source_target_pairs={{0,8},{2,10},{4,12},{6,14},{8,0},{10,2},{12,4},{14,6},{1,9},{3,11}... | collective-permute-start | bytes 18440 | tf_op jit(solution)/shard_map/ppermute | solution.py:371
  34.8 8.6 %collective-permute-start.1 = (bf16[408,128]{1,0:T(8,128)(2,1)S(1)}, bf16[408,128]{1,0:T(8,128)(2,1)S(1)}, u32[]{:S(2)}, u32[]{:S(2)}) collective-permute-start(bf16[408,128]{1,0:T(8,128)(2,1)S(1)} %get-tuple-element.19), channel_id=1, source_target_pairs={{0,2},{2,4},{4,6},{6,8},{8,10},{10,12},{12,14},{14,0},{1,3},{3,5},... | collective-permute-start | bytes 313352 | tf_op jit(solution)/shard_map/ppermute | solution.py:369
  36.6 7.7 %collective-permute-start.2 = (bf16[408,128]{1,0:T(8,128)(2,1)S(1)}, bf16[408,128]{1,0:T(8,128)(2,1)S(1)}, u32[]{:S(2)}, u32[]{:S(2)}) collective-permute-start(bf16[408,128]{1,0:T(8,128)(2,1)S(1)} %get-tuple-element.20), channel_id=1, source_target_pairs={{0,4},{2,6},{4,8},{6,10},{8,12},{10,14},{12,0},{14,2},{1,5},{3,7},... | collective-permute-start | bytes 313352 | tf_op jit(solution)/shard_map/ppermute | solution.py:369
  38.4 9.7 %collective-permute-start.3 = (bf16[408,128]{1,0:T(8,128)(2,1)S(1)}, bf16[408,128]{1,0:T(8,128)(2,1)S(1)}, u32[]{:S(2)}, u32[]{:S(2)}) collective-permute-start(bf16[408,128]{1,0:T(8,128)(2,1)S(1)} %get-tuple-element.21), channel_id=1, source_target_pairs={{0,6},{2,8},{4,10},{6,12},{8,14},{10,0},{12,2},{14,4},{1,7},{3,9},... | collective-permute-start | bytes 313352 | tf_op jit(solution)/shard_map/ppermute | solution.py:369
  43.4 8.5 %collective-permute-start.5 = (bf16[408,128]{1,0:T(8,128)(2,1)S(1)}, bf16[408,128]{1,0:T(8,128)(2,1)S(1)}, u32[]{:S(2)}, u32[]{:S(2)}) collective-permute-start(bf16[408,128]{1,0:T(8,128)(2,1)S(1)} %get-tuple-element.23), channel_id=1, source_target_pairs={{0,10},{2,12},{4,14},{6,0},{8,2},{10,4},{12,6},{14,8},{1,11},{3,13... | collective-permute-start | bytes 313352 | tf_op jit(solution)/shard_map/ppermute | solution.py:369
  44.3 7.7 %collective-permute-start.6 = (bf16[408,128]{1,0:T(8,128)(2,1)S(1)}, bf16[408,128]{1,0:T(8,128)(2,1)S(1)}, u32[]{:S(2)}, u32[]{:S(2)}) collective-permute-start(bf16[408,128]{1,0:T(8,128)(2,1)S(1)} %get-tuple-element.24), channel_id=1, source_target_pairs={{0,12},{2,14},{4,0},{6,2},{8,4},{10,6},{12,8},{14,10},{1,13},{3,15... | collective-permute-start | bytes 313352 | tf_op jit(solution)/shard_map/ppermute | solution.py:369
  48.1 6.1 %collective-permute-start.7 = (bf16[408,128]{1,0:T(8,128)(2,1)S(1)}, bf16[408,128]{1,0:T(8,128)(2,1)S(1)}, u32[]{:S(2)}, u32[]{:S(2)}) collective-permute-start(bf16[408,128]{1,0:T(8,128)(2,1)S(1)} %get-tuple-element.25), channel_id=1, source_target_pairs={{0,14},{2,0},{4,2},{6,4},{8,6},{10,8},{12,10},{14,12},{1,15},{3,1}... | collective-permute-start | bytes 313352 | tf_op jit(solution)/shard_map/ppermute | solution.py:369
  54.2 21.8 %copy-start.3 = (f32[1,1024]{1,0:T(1,128)S(1)}, f32[1,1024]{1,0:T(1,128)}, u32[]{:S(2)}) copy-start(f32[1,1024]{1,0:T(1,128)} %refl_ref.1) | copy-start | bytes 12292
  61.3 14.7 %all-to-all-start = ((f32[32,8,128]{2,1,0:T(8,128)}), f32[32,8,128]{2,1,0:T(8,128)S(1)}, u32[]{:S(2)}, u32[]{:S(2)}) async-start(f32[32,8,128]{2,1,0:T(8,128)} %bitcast.7), calls=%async_computation | async-start | bytes 262144 | tf_op jit(solution)/shard_map/all_to_all | solution.py:401

commit v2 on v1

--- a/solution.py
+++ b/solution.py
@@ -93,7 +93,7 @@
 
 
 ROWS_STEP = 4
-FAR = 1
+FAR = 2
 LANES = 128
 SUBLANES = 8
 HALF = LANES // 2
@@ -205,9 +205,14 @@
         count = jnp.broadcast_to(listed[:, 2 * slots:2 * slots + 1], (entries, LANES))
         tile = pltpu.roll(listed, LANES - slots, 1)
         place = jnp.where(lane < count, listed * entries + tile, float(blocks * entries))
-        index_buf[level] = (place * unit).astype(jnp.int32)
+        place = place * unit
+        if level:
+            placed = jnp.where(lane < HALF, placed, pltpu.roll(place, level * HALF, 1))
+        else:
+            placed = place
         scale = 1.0 / jnp.sqrt(count)
         factor_buf[level] = scale if level == levels - 1 else scale * factor_buf[level]
+    index_buf[...] = placed.astype(jnp.int32)
     index_copy = pltpu.make_async_copy(index_buf, index_ref, sem)
     index_copy.start()
     table[blocks * entries * unit:, :] = jnp.zeros((unit, LANES), jnp.float32)
@@ -267,7 +272,7 @@
                 row = step * ROWS_STEP + inner
                 total = None
                 for slot in range(slots):
-                    start = pl.multiple_of(index_ref[level, row, slot], SUBLANES)
+                    start = pl.multiple_of(index_ref[row, level * HALF + slot], SUBLANES)
                     term = table[pl.ds(start, unit), :]
                     total = term if total is None else total + term
                 total = total * factor_buf[level, pl.ds(row, 1), :]
@@ -292,7 +297,7 @@
                     ).astype(jnp.bfloat16)
             return carry
 
-        lax.fori_loop(0, entries // ROWS_STEP, row_step, 0)
+        lax.fori_loop(0, entries // ROWS_STEP, row_step, 0, unroll=2)
 
     summed = jnp.sum(squares_buf[...], axis=1)
     for level in range(levels):
@@ -303,7 +308,7 @@
 
 
 def turns_of(lat_size):
-    turns = sorted(range(1, lat_size), key=lambda turn: abs(turn - lat_size // 2))
+    turns = sorted(range(1, lat_size), key=lambda turn: (abs(turn - lat_size // 2), -turn))
     return turns[:FAR], turns[FAR:]
 
 
@@ -385,8 +390,8 @@
             pltpu.VMEM((levels * entries, SUBLANES, LANES), jnp.float32),
             pltpu.VMEM((entries, LANES), jnp.float32),
             pltpu.VMEM((levels, entries, LANES), jnp.float32),
-            pltpu.VMEM((levels, entries, LANES), jnp.int32),
-            pltpu.SMEM((levels, entries, LANES), jnp.int32),
+            pltpu.VMEM((entries, LANES), jnp.int32),
+            pltpu.SMEM((entries, LANES), jnp.int32),
             pltpu.SemaphoreType.DMA,
         ],
         cost_estimate=pl.CostEstimate(

time: 76.9 us -> 78.9 us (1.026)
  waiting for transfers between devices: 35.6 us -> 37.6 us
    ppermute x1 -> x2, waiting for transfers between devices: 0.01 us -> 4.95 us  [per_device_fast(): waves[turn] = lax.ppermute(chunk, 'lat', around(turn))]
    ppermute x6 -> x5, waiting for transfers between devices: 8.29 us -> 3.4 us  [per_device_fast(): tails[turn] = waves[turn] = lax.ppermute(chunk, 'lat', around(turn))]
    ppermute x6 -> x5, starting transfers between devices: 10.9 us -> 8.92 us  [per_device_fast(): tails[turn] = waves[turn] = lax.ppermute(chunk, 'lat', around(turn))]
    ppermute x1 -> x2, waiting for transfers between devices: 0.23 us -> 2.14 us  [per_device_fast(): tails[turn] = lax.ppermute(lists, 'lat', around(turn))]
    ppermute x1 -> x2, starting transfers between devices: 3.01 us -> 4.91 us  [per_device_fast(): waves[turn] = lax.ppermute(chunk, 'lat', around(turn))]
    ppermute x1 -> x2, starting transfers between devices: 2.87 us -> 4.13 us  [per_device_fast(): tails[turn] = lax.ppermute(lists, 'lat', around(turn))]
    all_to_all x1, starting transfers between devices: 6.45 us -> 5.3 us  [per_device_fast(): parts = lax.all_to_all(spread, ('depth', 'lat', 'freq'), 0, 0, tiled=True)]
  transfers between devices with their start and end apart: 12 -> 13, of which waited for: 7 -> 8; matrix products, arithmetic and copies ran while one was open for 0% -> 0% of each run, Pallas kernels for 2% -> 2%
where the time goes in v2:
time: 78.9 us; the launch traced here: 78.6 us
  waiting for transfers between devices  37.6 us (48%)
  starting transfers between devices  27.9 us (35%)
  Pallas kernels  11.6 us (15%)
    ppermute x1, waiting for transfers between devices, per_device_fast(): other = lax.ppermute(mine, 'depth', swap)  18.9 us
    ppermute x5, starting transfers between devices, per_device_fast(): tails[turn] = waves[turn] = lax.ppermute(chunk, 'lat', around(turn))  8.92 us
    all_to_all x1, waiting for transfers between devices, per_device_fast(): parts = lax.all_to_all(spread, ('depth', 'lat', 'freq'), 0, 0, tiled=True)  8.2 us
    pallas_call x1, Pallas kernels, per_device_fast(): pl.pallas_call(functools.partial(level_kernel, lat_size, freq_size, slots...  7.1 us
    all_to_all x1, starting transfers between devices, per_device_fast(): parts = lax.all_to_all(spread, ('depth', 'lat', 'freq'), 0, 0, tiled=True)  5.3 us
    ppermute x2, waiting for transfers between devices, per_device_fast(): waves[turn] = lax.ppermute(chunk, 'lat', around(turn))  4.95 us
    ppermute x2, starting transfers between devices, per_device_fast(): waves[turn] = lax.ppermute(chunk, 'lat', around(turn))  4.91 us
    ppermute x2, starting transfers between devices, per_device_fast(): tails[turn] = lax.ppermute(lists, 'lat', around(turn))  4.13 us
  transfers between devices with their start and end apart: 13, of which 8 were waited for; matrix products, arithmetic and copies ran while one was open for 0% of the time, Pallas kernels for 2%

profile of v2, /device:TPU:0, one launch (start us, length us, event | category | flops | bytes accessed | tf_op | source)
XLA Modules:
  0.0 78.6 jit_solution(2083572343860859762)
XLA Ops:
  0.0 3.3 %first.1 = (f32[16,128]{1,0:T(8,128)}, bf16[8,128,256]{2,1,0:T(8,128)(2,1)}, bf16[8,128,256]{2,1,0:T(8,128)(2,1)}, bf16[384,128]{1,0:T(8,128)(2,1)}, bf16[384,128]{1,0:T(8,128)(2,1)}) custom-call(s32[1]{0:T(128)} %bitcast.depth_ref, s32[1]{0:T(128)} %bitcast.1.lat_ref, bf16[3,2,16,64,128]{4,3,2,1,0:T(8,128)(2,1)} %bitcast.9, ...), custom_call_target="tpu_custom_call" | custom-call | tf_op jit(solution)/shard_map/first/pallas_call | solution.py:345
  3.3 0.0 copy-start.1
  3.3 3.1 %collective-permute-start.10 = (bf16[8,128,256]{2,1,0:T(8,128)(2,1)}, bf16[8,128,256]{2,1,0:T(8,128)(2,1)S(1)}, u32[]{:S(2)}, u32[]{:S(2)}) collective-permute-start(bf16[8,128,256]{2,1,0:T(8,128)(2,1)} %get-tuple-element.27), channel_id=1, source_target_pairs={{0,16},{16,0},{1,17},{17,1},{2,18},{18,2},{3,19},{19,3},{4,20},{20... | collective-permute-start | bytes 1572872 | tf_op jit(solution)/shard_map/ppermute | solution.py:355
  6.4 0.1 collective-permute-start.11
  6.4 3.0 %collective-permute-start.4 = (bf16[384,128]{1,0:T(8,128)(2,1)}, bf16[384,128]{1,0:T(8,128)(2,1)S(1)}, u32[]{:S(2)}, u32[]{:S(2)}) collective-permute-start(bf16[384,128]{1,0:T(8,128)(2,1)} %get-tuple-element.22), channel_id=1, source_target_pairs={{0,8},{2,10},{4,12},{6,14},{8,0},{10,2},{12,4},{14,6},{1,9},{3,11}... | collective-permute-start | bytes 294920 | tf_op jit(solution)/shard_map/ppermute | solution.py:363
  9.5 1.5 %collective-permute-start = (f32[16,128]{1,0:T(8,128)}, f32[16,128]{1,0:T(8,128)S(1)}, u32[]{:S(2)}, u32[]{:S(2)}) collective-permute-start(f32[16,128]{1,0:T(8,128)} %get-tuple-element.17.mine_ref), channel_id=1, source_target_pairs={{0,16},{16,0},{1,17},{17,1},{2,18},{18,2},{3,19},{19,3},{4,20},{20... | collective-permute-start | bytes 24584 | tf_op jit(solution)/shard_map/ppermute | solution.py:354
  11.0 18.9 %collective-permute-done.other_ref = f32[16,128]{1,0:T(8,128)S(1)} collective-permute-done((f32[16,128]{1,0:T(8,128)}, f32[16,128]{1,0:T(8,128)S(1)}, u32[]{:S(2)}, u32[]{:S(2)}) %collective-permute-start) | collective-permute-done | bytes 8224 | tf_op jit(solution)/shard_map/ppermute | solution.py:354
  29.9 0.7 copy-done.2
  30.6 1.2 %second.1 = (bf16[408,128]{1,0:T(8,128)(2,1)S(1)}, bf16[408,128]{1,0:T(8,128)(2,1)S(1)}, bf16[408,128]{1,0:T(8,128)(2,1)S(1)}, bf16[408,128]{1,0:T(8,128)(2,1)S(...) custom-call(s32[1]{0:T(128)} %bitcast.depth_ref, s32[1]{0:T(128)} %bitcast.1.lat_ref, ...), custom_call_target="tpu_custom_call" | custom-call | tf_op jit(solution)/shard_map/second/pallas_call | solution.py:364
  31.8 3.8 %collective-permute-start.9 = (bf16[24,128]{1,0:T(8,128)(2,1)S(1)}, bf16[24,128]{1,0:T(8,128)(2,1)S(1)}, u32[]{:S(2)}, u32[]{:S(2)}) collective-permute-start(bf16[24,128]{1,0:T(8,128)(2,1)S(1)} %get-tuple-element.26), channel_id=1, source_target_pairs={{0,10},{2,12},{4,14},{6,0},{8,2},{10,4},{12,6},{14,8},{1,11},{3,13... | collective-permute-start | bytes 18440 | tf_op jit(solution)/shard_map/ppermute | solution.py:376
  35.6 0.3 collective-permute-start.8
  36.0 1.0 %collective-permute-done.9.refs_13_ = bf16[24,128]{1,0:T(8,128)(2,1)S(1)} collective-permute-done((bf16[24,128]{1,0:T(8,128)(2,1)S(1)}, bf16[24,128]{1,0:T(8,128)(2,1)S(1)}, u32[]{:S(2)}, u32[]{:S(2)}) %collective-permute-start.9) | collective-permute-done | bytes 6176 | tf_op jit(solution)/shard_map/ppermute | solution.py:376
  37.0 2.1 %collective-permute-start.1 = (bf16[408,128]{1,0:T(8,128)(2,1)S(1)}, bf16[408,128]{1,0:T(8,128)(2,1)S(1)}, u32[]{:S(2)}, u32[]{:S(2)}) collective-permute-start(bf16[408,128]{1,0:T(8,128)(2,1)S(1)} %get-tuple-element.19), channel_id=1, source_target_pairs={{0,2},{2,4},{4,6},{6,8},{8,10},{10,12},{12,14},{14,0},{1,3},{3,5},... | collective-permute-start | bytes 313352 | tf_op jit(solution)/shard_map/ppermute | solution.py:374
  39.0 1.1 %collective-permute-done.8.refs_12_ = bf16[24,128]{1,0:T(8,128)(2,1)S(1)} collective-permute-done((bf16[24,128]{1,0:T(8,128)(2,1)S(1)}, bf16[24,128]{1,0:T(8,128)(2,1)S(1)}, u32[]{:S(2)}, u32[]{:S(2)}) %collective-permute-start.8) | collective-permute-done | bytes 6176 | tf_op jit(solution)/shard_map/ppermute | solution.py:376
  40.1 1.6 %collective-permute-start.2 = (bf16[408,128]{1,0:T(8,128)(2,1)S(1)}, bf16[408,128]{1,0:T(8,128)(2,1)S(1)}, u32[]{:S(2)}, u32[]{:S(2)}) collective-permute-start(bf16[408,128]{1,0:T(8,128)(2,1)S(1)} %get-tuple-element.20), channel_id=1, source_target_pairs={{0,4},{2,6},{4,8},{6,10},{8,12},{10,14},{12,0},{14,2},{1,5},{3,7},... | collective-permute-start | bytes 313352 | tf_op jit(solution)/shard_map/ppermute | solution.py:374
  41.7 0.0 collective-permute-done.4.refs_4_
  41.7 1.9 %collective-permute-start.5 = (bf16[384,128]{1,0:T(8,128)(2,1)}, bf16[384,128]{1,0:T(8,128)(2,1)S(1)}, u32[]{:S(2)}, u32[]{:S(2)}) collective-permute-start(bf16[384,128]{1,0:T(8,128)(2,1)} %get-tuple-element.23), channel_id=1, source_target_pairs={{0,10},{2,12},{4,14},{6,0},{8,2},{10,4},{12,6},{14,8},{1,11},{3,13... | collective-permute-start | bytes 294920 | tf_op jit(solution)/shard_map/ppermute | solution.py:363
  43.6 5.0 %collective-permute-done.5.refs_5_ = bf16[384,128]{1,0:T(8,128)(2,1)S(1)} collective-permute-done((bf16[384,128]{1,0:T(8,128)(2,1)}, bf16[384,128]{1,0:T(8,128)(2,1)S(1)}, u32[]{:S(2)}, u32[]{:S(2)}) %collective-permute-start.5) | collective-permute-done | bytes 98336 | tf_op jit(solution)/shard_map/ppermute | solution.py:363
  48.6 2.6 %collective-permute-start.3 = (bf16[408,128]{1,0:T(8,128)(2,1)S(1)}, bf16[408,128]{1,0:T(8,128)(2,1)S(1)}, u32[]{:S(2)}, u32[]{:S(2)}) collective-permute-start(bf16[408,128]{1,0:T(8,128)(2,1)S(1)} %get-tuple-element.21), channel_id=1, source_target_pairs={{0,6},{2,8},{4,10},{6,12},{8,14},{10,0},{12,2},{14,4},{1,7},{3,9},... | collective-permute-start | bytes 313352 | tf_op jit(solution)/shard_map/ppermute | solution.py:374
  51.2 0.0 collective-permute-done.1.refs_1_.refs_9_
  51.2 1.2 %collective-permute-start.6 = (bf16[408,128]{1,0:T(8,128)(2,1)S(1)}, bf16[408,128]{1,0:T(8,128)(2,1)S(1)}, u32[]{:S(2)}, u32[]{:S(2)}) collective-permute-start(bf16[408,128]{1,0:T(8,128)(2,1)S(1)} %get-tuple-element.24), channel_id=1, source_target_pairs={{0,12},{2,14},{4,0},{6,2},{8,4},{10,6},{12,8},{14,10},{1,13},{3,15... | collective-permute-start | bytes 313352 | tf_op jit(solution)/shard_map/ppermute | solution.py:374
  52.4 0.0 collective-permute-done.2.refs_2_.refs_10_
  52.4 1.4 %collective-permute-start.7 = (bf16[408,128]{1,0:T(8,128)(2,1)S(1)}, bf16[408,128]{1,0:T(8,128)(2,1)S(1)}, u32[]{:S(2)}, u32[]{:S(2)}) collective-permute-start(bf16[408,128]{1,0:T(8,128)(2,1)S(1)} %get-tuple-element.25), channel_id=1, source_target_pairs={{0,14},{2,0},{4,2},{6,4},{8,6},{10,8},{12,10},{14,12},{1,15},{3,1}... | collective-permute-start | bytes 313352 | tf_op jit(solution)/shard_map/ppermute | solution.py:374
  53.9 2.4 %collective-permute-done.3.refs_3_.refs_11_ = bf16[408,128]{1,0:T(8,128)(2,1)S(1)} collective-permute-done((bf16[408,128]{1,0:T(8,128)(2,1)S(1)}, bf16[408,128]{1,0:T(8,128)(2,1)S(1)}, u32[]{:S(2)}, u32[]{:S(2)}) %collective-permute-start.3) | collective-permute-done | bytes 104480 | tf_op jit(solution)/shard_map/ppermute | solution.py:374
  56.3 0.1 collective-permute-done.6.refs_6_.refs_14_
  56.4 0.9 %collective-permute-done.7.refs_7_.refs_15_ = bf16[408,128]{1,0:T(8,128)(2,1)S(1)} collective-permute-done((bf16[408,128]{1,0:T(8,128)(2,1)S(1)}, bf16[408,128]{1,0:T(8,128)(2,1)S(1)}, u32[]{:S(2)}, u32[]{:S(2)}) %collective-permute-start.7) | collective-permute-done | bytes 104480 | tf_op jit(solution)/shard_map/ppermute | solution.py:374
  57.3 0.0 collective-permute-done.10.refs_17_
  57.3 0.0 copy-start.3
  57.3 7.1 %levels.1 = f32[2,8,2,8,128]{4,3,2,1,0:T(8,128)} custom-call(s32[1]{0:T(128)} %bitcast.depth_ref, s32[1]{0:T(128)} %bitcast.1.lat_ref, bf16[408,128]{1,0:T(8,128)(2,1)S(1)} %get-tuple-element.18.refs_0_.refs_8_, bf16[408,128]{1,0:T(8,128)(2,1)S(1)} %collective-permute-done.1.refs_1_.refs_9_, bf16[408,128]{1,0:T(8,128)(2,1)S(1)} %collective-permute-done.2.refs_2_.refs_10_, ...), custom_call_target="tpu_custom_call" | custom-call | flops 3221225472 | bytes 2883584 | tf_op jit(solution)/shard_map/levels/pallas_call | solution.py:381
  64.4 5.3 %all-to-all-start = ((f32[32,8,128]{2,1,0:T(8,128)}), f32[32,8,128]{2,1,0:T(8,128)S(1)}, u32[]{:S(2)}, u32[]{:S(2)}) async-start(f32[32,8,128]{2,1,0:T(8,128)} %bitcast.7), calls=%async_computation | async-start | bytes 262144 | tf_op jit(solution)/shard_map/all_to_all | solution.py:406
  69.7 8.2 %all-to-all-done = f32[32,8,128]{2,1,0:T(8,128)S(1)} async-done(((f32[32,8,128]{2,1,0:T(8,128)}), f32[32,8,128]{2,1,0:T(8,128)S(1)}, u32[]{:S(2)}, u32[]{:S(2)}) %all-to-all-start) | async-done | bytes 131104 | tf_op jit(solution)/shard_map/all_to_all | solution.py:406
  78.0 0.6 fusion.1
  (7 shorter events, 0.0 us)
Async XLA Ops:
  0.0 29.9 %copy-start = (bf16[3,2,128,1024]{3,2,1,0:T(8,128)(2,1)S(1)}, bf16[3,2,128,1024]{3,2,1,0:T(8,128)(2,1)}, u32[]{:S(2)}) copy-start(bf16[3,2,128,1024]{3,2,1,0:T(8,128)(2,1)} %param.6) | copy-start | bytes 4718596
  3.3 54.0 %copy-start.1 = (bf16[1,3,8,128,256]{4,3,2,1,0:T(8,128)(2,1)S(1)}, bf16[1,3,8,128,256]{4,3,2,1,0:T(8,128)(2,1)}, u32[]{:S(2)}) copy-start(bf16[1,3,8,128,256]{4,3,2,1,0:T(8,128)(2,1)} %refs_16_.1) | copy-start | bytes 4718596
  3.3 54.0 %collective-permute-start.10 = (bf16[8,128,256]{2,1,0:T(8,128)(2,1)}, bf16[8,128,256]{2,1,0:T(8,128)(2,1)S(1)}, u32[]{:S(2)}, u32[]{:S(2)}) collective-permute-start(bf16[8,128,256]{2,1,0:T(8,128)(2,1)} %get-tuple-element.27), channel_id=1, source_target_pairs={{0,16},{16,0},{1,17},{17,1},{2,18},{18,2},{3,19},{19,3},{4,20},{20... | collective-permute-start | bytes 1572872 | tf_op jit(solution)/shard_map/ppermute | solution.py:355
  6.4 50.9 %collective-permute-start.11 = (bf16[8,128,256]{2,1,0:T(8,128)(2,1)}, bf16[8,128,256]{2,1,0:T(8,128)(2,1)S(1)}, u32[]{:S(2)}, u32[]{:S(2)}) collective-permute-start(bf16[8,128,256]{2,1,0:T(8,128)(2,1)} %get-tuple-element.28), channel_id=1, source_target_pairs={{0,16},{16,0},{1,17},{17,1},{2,18},{18,2},{3,19},{19,3},{4,20},{20... | collective-permute-start | bytes 1572872 | tf_op jit(solution)/shard_map/ppermute | solution.py:356
  6.4 35.3 %collective-permute-start.4 = (bf16[384,128]{1,0:T(8,128)(2,1)}, bf16[384,128]{1,0:T(8,128)(2,1)S(1)}, u32[]{:S(2)}, u32[]{:S(2)}) collective-permute-start(bf16[384,128]{1,0:T(8,128)(2,1)} %get-tuple-element.22), channel_id=1, source_target_pairs={{0,8},{2,10},{4,12},{6,14},{8,0},{10,2},{12,4},{14,6},{1,9},{3,11}... | collective-permute-start | bytes 294920 | tf_op jit(solution)/shard_map/ppermute | solution.py:363
  9.5 20.4 %collective-permute-start = (f32[16,128]{1,0:T(8,128)}, f32[16,128]{1,0:T(8,128)S(1)}, u32[]{:S(2)}, u32[]{:S(2)}) collective-permute-start(f32[16,128]{1,0:T(8,128)} %get-tuple-element.17.mine_ref), channel_id=1, source_target_pairs={{0,16},{16,0},{1,17},{17,1},{2,18},{18,2},{3,19},{19,3},{4,20},{20... | collective-permute-start | bytes 24584 | tf_op jit(solution)/shard_map/ppermute | solution.py:354
  29.9 0.7 copy-start.2
  31.8 5.1 %collective-permute-start.9 = (bf16[24,128]{1,0:T(8,128)(2,1)S(1)}, bf16[24,128]{1,0:T(8,128)(2,1)S(1)}, u32[]{:S(2)}, u32[]{:S(2)}) collective-permute-start(bf16[24,128]{1,0:T(8,128)(2,1)S(1)} %get-tuple-element.26), channel_id=1, source_target_pairs={{0,10},{2,12},{4,14},{6,0},{8,2},{10,4},{12,6},{14,8},{1,11},{3,13... | collective-permute-start | bytes 18440 | tf_op jit(solution)/shard_map/ppermute | solution.py:376
  35.6 4.5 %collective-permute-start.8 = (bf16[24,128]{1,0:T(8,128)(2,1)S(1)}, bf16[24,128]{1,0:T(8,128)(2,1)S(1)}, u32[]{:S(2)}, u32[]{:S(2)}) collective-permute-start(bf16[24,128]{1,0:T(8,128)(2,1)S(1)} %get-tuple-element.26), channel_id=1, source_target_pairs={{0,8},{2,10},{4,12},{6,14},{8,0},{10,2},{12,4},{14,6},{1,9},{3,11}... | collective-permute-start | bytes 18440 | tf_op jit(solution)/shard_map/ppermute | solution.py:376
  37.0 14.2 %collective-permute-start.1 = (bf16[408,128]{1,0:T(8,128)(2,1)S(1)}, bf16[408,128]{1,0:T(8,128)(2,1)S(1)}, u32[]{:S(2)}, u32[]{:S(2)}) collective-permute-start(bf16[408,128]{1,0:T(8,128)(2,1)S(1)} %get-tuple-element.19), channel_id=1, source_target_pairs={{0,2},{2,4},{4,6},{6,8},{8,10},{10,12},{12,14},{14,0},{1,3},{3,5},... | collective-permute-start | bytes 313352 | tf_op jit(solution)/shard_map/ppermute | solution.py:374
  40.1 12.3 %collective-permute-start.2 = (bf16[408,128]{1,0:T(8,128)(2,1)S(1)}, bf16[408,128]{1,0:T(8,128)(2,1)S(1)}, u32[]{:S(2)}, u32[]{:S(2)}) collective-permute-start(bf16[408,128]{1,0:T(8,128)(2,1)S(1)} %get-tuple-element.20), channel_id=1, source_target_pairs={{0,4},{2,6},{4,8},{6,10},{8,12},{10,14},{12,0},{14,2},{1,5},{3,7},... | collective-permute-start | bytes 313352 | tf_op jit(solution)/shard_map/ppermute | solution.py:374
  41.7 6.8 %collective-permute-start.5 = (bf16[384,128]{1,0:T(8,128)(2,1)}, bf16[384,128]{1,0:T(8,128)(2,1)S(1)}, u32[]{:S(2)}, u32[]{:S(2)}) collective-permute-start(bf16[384,128]{1,0:T(8,128)(2,1)} %get-tuple-element.23), channel_id=1, source_target_pairs={{0,10},{2,12},{4,14},{6,0},{8,2},{10,4},{12,6},{14,8},{1,11},{3,13... | collective-permute-start | bytes 294920 | tf_op jit(solution)/shard_map/ppermute | solution.py:363
  48.6 7.7 %collective-permute-start.3 = (bf16[408,128]{1,0:T(8,128)(2,1)S(1)}, bf16[408,128]{1,0:T(8,128)(2,1)S(1)}, u32[]{:S(2)}, u32[]{:S(2)}) collective-permute-start(bf16[408,128]{1,0:T(8,128)(2,1)S(1)} %get-tuple-element.21), channel_id=1, source_target_pairs={{0,6},{2,8},{4,10},{6,12},{8,14},{10,0},{12,2},{14,4},{1,7},{3,9},... | collective-permute-start | bytes 313352 | tf_op jit(solution)/shard_map/ppermute | solution.py:374
  51.2 5.2 %collective-permute-start.6 = (bf16[408,128]{1,0:T(8,128)(2,1)S(1)}, bf16[408,128]{1,0:T(8,128)(2,1)S(1)}, u32[]{:S(2)}, u32[]{:S(2)}) collective-permute-start(bf16[408,128]{1,0:T(8,128)(2,1)S(1)} %get-tuple-element.24), channel_id=1, source_target_pairs={{0,12},{2,14},{4,0},{6,2},{8,4},{10,6},{12,8},{14,10},{1,13},{3,15... | collective-permute-start | bytes 313352 | tf_op jit(solution)/shard_map/ppermute | solution.py:374
  52.4 4.8 %collective-permute-start.7 = (bf16[408,128]{1,0:T(8,128)(2,1)S(1)}, bf16[408,128]{1,0:T(8,128)(2,1)S(1)}, u32[]{:S(2)}, u32[]{:S(2)}) collective-permute-start(bf16[408,128]{1,0:T(8,128)(2,1)S(1)} %get-tuple-element.25), channel_id=1, source_target_pairs={{0,14},{2,0},{4,2},{6,4},{8,6},{10,8},{12,10},{14,12},{1,15},{3,1}... | collective-permute-start | bytes 313352 | tf_op jit(solution)/shard_map/ppermute | solution.py:374
  57.3 20.7 %copy-start.3 = (f32[1,1024]{1,0:T(1,128)S(1)}, f32[1,1024]{1,0:T(1,128)}, u32[]{:S(2)}) copy-start(f32[1,1024]{1,0:T(1,128)} %refl_ref.1) | copy-start | bytes 12292
  64.4 13.5 %all-to-all-start = ((f32[32,8,128]{2,1,0:T(8,128)}), f32[32,8,128]{2,1,0:T(8,128)S(1)}, u32[]{:S(2)}, u32[]{:S(2)}) async-start(f32[32,8,128]{2,1,0:T(8,128)} %bitcast.7), calls=%async_computation | async-start | bytes 262144 | tf_op jit(solution)/shard_map/all_to_all | solution.py:406
